TPU v7x, 32 devices: a whole 2x2x4 slice. The times are simulated.
32 devices in a mesh: rep: 2 (over core), row: 4 (over y, x), col: 4 (over z).
Axes of the slice: x: 2, y: 2, z: 4, core: 2. Of those that a mesh axis runs over, the one named last changes fastest.
Arguments:
- velocity: bfloat16 [6, 16, 512, 512], P('rep', 'col', 'row'), parts along dimension 0, may hold values from -6 to 6
- target: bfloat16 [6, 16, 512, 512], P('rep', 'col', 'row'), parts along dimension 0, may hold values from -6 to 6
- w_in: bfloat16 [9, 64], replicated, may hold values from -2 to 2
- w_out: bfloat16 [6, 64], replicated, may hold values from -0.75 to 0.75
- diff_x: bfloat16 [512, 512], replicated, may hold values from -3 to 3, as said below
- diff_y: bfloat16 [512, 512], replicated, may hold values from -3 to 3, as said below
- metric_z: float32 [16], replicated, may hold values from 0.5 to 2
Outputs:
- new_velocity: bfloat16 [6, 16, 512, 512], P('rep', 'col', 'row'), parts along dimension 0
- grad_w_in: float32 [18, 64], P('rep'), parts along dimension 0
- grad_w_out: float32 [12, 64], P('rep'), parts along dimension 0
There are 2 independent parts, one for each index of `rep`. A program takes and returns all parts, laid end to end along the dimension named above; an argument that names none is the same for every part. Nothing has to cross between parts.
Inputs may be any that keep to these rules, and one draw needn't show every extreme that they name: `diff_x`: a dense first derivative matrix of the stretched mesh along x. `diff_y`: a dense first derivative matrix of the stretched mesh along y.
All inputs are finite; a program needn't handle non-finite values.
Results may differ from a plain program's by a relative error of at most 0.0037.
Values may be sent and summed in bfloat16 or wider, within the bound.
A program may use at most 128 MiB of HBM per device.

v0:
```python
import math

import jax
import jax.numpy as jnp
from jax import lax
from jax.sharding import PartitionSpec as P

COEFS = (0.75, -0.15, 1.0 / 60.0)
STEP_SIZE = 0.3


def padded_2(cells, sides, width):
    for axis, dim in sides:
        count = lax.axis_size(axis)
        head = lax.slice_in_dim(cells, 0, width, axis=dim)
        tail = lax.slice_in_dim(cells, cells.shape[dim] - width, cells.shape[dim], axis=dim)
        cells = jnp.concatenate(
            [
                lax.ppermute(tail, axis, [(i, (i + 1) % count) for i in range(count)]),
                cells,
                lax.ppermute(head, axis, [((i + 1) % count, i) for i in range(count)]),
            ],
            axis=dim,
        )
    return cells


def features_of(center, left_side, right_side):
    return jnp.concatenate([left_side, center, right_side], 0).reshape(9, -1)


def closure_forward(features, w_in, w_out):
    preact = jnp.dot(w_in.T, features, preferred_element_type=jnp.float32)
    hidden = (preact * jax.nn.sigmoid(preact)).astype(jnp.bfloat16)
    return jnp.dot(w_out, hidden, preferred_element_type=jnp.float32).astype(jnp.bfloat16)


def closure_backward(features, upstream, w_in, w_out):
    preact = jnp.dot(w_in.T, features, preferred_element_type=jnp.float32)
    sigmoid_val = jax.nn.sigmoid(preact)
    hidden = (preact * sigmoid_val).astype(jnp.bfloat16)
    grad_out = lax.dot_general(
        upstream, hidden, (((1,), (1,)), ((), ())), preferred_element_type=jnp.float32
    )
    back_hidden = jnp.dot(w_out.T, upstream, preferred_element_type=jnp.float32)
    back_pre = (back_hidden * sigmoid_val * (1.0 + preact * (1.0 - sigmoid_val))).astype(
        jnp.bfloat16
    )
    grad_in = lax.dot_general(
        features, back_pre, (((1,), (1,)), ((), ())), preferred_element_type=jnp.float32
    )
    return (grad_in, grad_out)


def plane_stencil(padded, z_cells):
    total = jnp.zeros(padded.shape[:1] + (z_cells,) + padded.shape[2:], jnp.float32)
    for reach in (1, 2, 3):
        total = total + COEFS[reach - 1] * (
            padded[:, 3 + reach : 3 + reach + z_cells] - padded[:, 3 - reach : 3 - reach + z_cells]
        )
    return total


def along_y(matrix_y, field, pattern):
    return jnp.einsum(pattern, matrix_y, field, preferred_element_type=jnp.float32)


def local(velocity, target, w_in, w_out, diff_x, diff_y, metric_z):
    z_cells = velocity.shape[1]
    y_local = velocity.shape[2]
    x_cells = velocity.shape[3]
    y_total = diff_y.shape[0]
    z_total = metric_z.shape[0]
    nblocks = math.gcd(4, z_cells)
    planes_blk = z_cells // nblocks

    def to_blocks(array):
        return jnp.moveaxis(
            array.reshape(array.shape[0], nblocks, planes_blk, y_local, x_cells), 1, 0
        )

    def tau_block(slab):
        feats = features_of(slab, jnp.roll(slab, 1, axis=3), jnp.roll(slab, -1, axis=3))
        return closure_forward(feats, w_in, w_out).reshape(6, planes_blk, y_local, x_cells)

    pencil = lax.all_to_all(velocity, "row", split_axis=3, concat_axis=2, tiled=True)
    velocity_halo = padded_2(velocity, (("col", 1),), 3)
    velocity_pad = velocity_halo.astype(jnp.float32)
    stress = jnp.moveaxis(lax.map(tau_block, to_blocks(velocity)), 0, 1).reshape(
        6, z_cells, y_local, x_cells
    )
    stress_x = jnp.stack([stress[0], stress[3], stress[4]])
    stress_z = jnp.stack([stress[4], stress[5], stress[2]])
    vel_wide = velocity.astype(jnp.float32)
    start_cell = lax.axis_index("col") * z_cells
    tripled = jnp.concatenate([metric_z, metric_z, metric_z])
    metric_ext = lax.dynamic_slice_in_dim(tripled, start_cell + z_total - 3, z_cells + 6)[
        None, :, None, None
    ]
    metric_here = metric_ext[:, 3 : 3 + z_cells]
    pencil_deriv = along_y(diff_y, pencil, "ky,czyx->czkx")
    stress_y = jnp.stack([stress[3], stress[1], stress[5]])
    stress_pencil = lax.all_to_all(stress_y, "row", split_axis=3, concat_axis=2, tiled=True)
    combined = (
        along_y(diff_y, stress_pencil, "ky,czyx->czkx")
        + pencil[1:2].astype(jnp.float32) * pencil_deriv
    )
    dims_x = (((3,), (1,)), ((), ()))
    part_x = lax.dot_general(stress_x, diff_x, dims_x, preferred_element_type=jnp.float32)
    part_x = part_x + vel_wide[0:1] * lax.dot_general(
        velocity, diff_x, dims_x, preferred_element_type=jnp.float32
    )
    stress_pad = padded_2(stress_z, (("col", 1),), 3).astype(jnp.float32)
    part_z = metric_here * plane_stencil(stress_pad, z_cells) + vel_wide[2:3] * (
        metric_here * plane_stencil(velocity_pad, z_cells)
    )
    part_y = lax.all_to_all(
        combined.astype(jnp.bfloat16), "row", split_axis=2, concat_axis=3, tiled=True
    )
    advanced = vel_wide - STEP_SIZE * (part_x + part_y.astype(jnp.float32) + part_z)
    new_velocity = advanced.astype(jnp.bfloat16)
    residual = (advanced - target.astype(jnp.float32)).astype(jnp.bfloat16)
    backward = along_y(
        diff_y,
        lax.all_to_all(residual, "row", split_axis=3, concat_axis=2, tiled=True),
        "ky,czkx->czyx",
    ).astype(jnp.bfloat16)
    adj_y = lax.all_to_all(backward, "row", split_axis=2, concat_axis=3, tiled=True).astype(
        jnp.float32
    )
    adj_x = lax.dot_general(
        residual, diff_x, (((3,), (0,)), ((), ())), preferred_element_type=jnp.float32
    )
    residual_pad = padded_2(residual, (("col", 1),), 3)
    weighted = residual_pad.astype(jnp.float32) * metric_ext
    adj_z = -plane_stencil(weighted, z_cells)
    scale = -STEP_SIZE / math.sqrt(x_cells * y_total * z_total)
    upstream = (
        scale
        * jnp.stack(
            [
                adj_x[0],
                adj_y[1],
                adj_z[2],
                adj_x[1] + adj_y[0],
                adj_x[2] + adj_z[0],
                adj_y[2] + adj_z[1],
            ]
        )
    ).astype(jnp.bfloat16)

    def accumulate(carry, pair):
        slab, slab_up = pair
        feats = features_of(slab, jnp.roll(slab, 1, axis=3), jnp.roll(slab, -1, axis=3))
        grad_in, grad_out = closure_backward(feats, slab_up.reshape(6, -1), w_in, w_out)
        return ((carry[0] + grad_in, carry[1] + grad_out), None)

    channels = w_in.shape[1]
    start_val = (jnp.zeros((9, channels), jnp.float32), jnp.zeros((6, channels), jnp.float32))
    totals, unused = lax.scan(accumulate, start_val, (to_blocks(velocity), to_blocks(upstream)))
    grad_w_in, grad_w_out = lax.psum((totals[0], totals[1]), ("row", "col"))
    return (new_velocity, grad_w_in, grad_w_out)


def solution(mesh):
    return jax.shard_map(
        local,
        mesh=mesh,
        in_specs=(
            P("rep", "col", "row", None),
            P("rep", "col", "row", None),
            P(),
            P(),
            P(),
            P(),
            P(),
        ),
        out_specs=(P("rep", "col", "row", None), P("rep", None), P("rep", None)),
        check_vma=False,
    )
```

profile of v0, /device:TPU:0, one launch (start us, length us, event | category | flops | bytes accessed | tf_op | source)
XLA Modules:
  0.0 541.8 jit_solution(15487841160895617559)
XLA Ops:
  11.3 59.5 %while.23 = (s32[]{:T(128)}, bf16[4,6,1,128,512]{4,3,0,2,1:T(8,128)(2,1)}, bf16[4,3,1,128,512]{4,3,2,1,0:T(8,128)(2,1)}, bf16[9,64]{1,0:T(8,128)(2,1)S(1)}, bf16[6,64]{1,0:T(8,128)(2,1)S(1)}, /*index=5*/s32[]{:T(128)}) while((s32[]{:T(128)}, bf16[4,6,1,128,512]{4,3,0,2,1:T(8,128)(2,1)}, bf16[4,3,1,128,512]{4,3,2,1,0:T(8,128)(2,1)}, ...), condition=%wide.region_1.2_spmd, body=%wide.region_0.1_spmd.sunk | while | flops 152305664 | bytes 10226121 | solution.py:89
  16.3 8.7 %convolution_convert_fusion.3 = bf16[65536,6]{0,1:T(8,128)(2,1)S(1)} fusion(bf16[6,64]{1,0:T(8,128)(2,1)S(1)} %get-tuple-element.295, bf16[9,64]{1,0:T(8,128)(2,1)S(1)} %get-tuple-element.294, bf16[3,65536]{1,0:T(4,128)(2,1)} %bitcast.245, bf16[3,65536]{1,0:T(4,128)(2,1)} %bitcast.247, bf16[3,65536]{1,0:T(4,128)(2,1)} %bitcast.246), kind=kOutput, calls=%fused_computation.1.clone.1 | convolution fusion | flops 150732800 | bytes 1968000 | tf_op jit(solution)/shard_map/while/body/eval_jaxpr/dot_general | solution.py:35
  31.2 8.7 %convolution_convert_fusion.3 = bf16[65536,6]{0,1:T(8,128)(2,1)S(1)} fusion(bf16[6,64]{1,0:T(8,128)(2,1)S(1)} %get-tuple-element.295, bf16[9,64]{1,0:T(8,128)(2,1)S(1)} %get-tuple-element.294, bf16[3,65536]{1,0:T(4,128)(2,1)} %bitcast.245, bf16[3,65536]{1,0:T(4,128)(2,1)} %bitcast.247, bf16[3,65536]{1,0:T(4,128)(2,1)} %bitcast.246), kind=kOutput, calls=%fused_computation.1.clone.1 | convolution fusion | flops 150732800 | bytes 1968000 | tf_op jit(solution)/shard_map/while/body/eval_jaxpr/dot_general | solution.py:35
  46.1 8.7 %convolution_convert_fusion.3 = bf16[65536,6]{0,1:T(8,128)(2,1)S(1)} fusion(bf16[6,64]{1,0:T(8,128)(2,1)S(1)} %get-tuple-element.295, bf16[9,64]{1,0:T(8,128)(2,1)S(1)} %get-tuple-element.294, bf16[3,65536]{1,0:T(4,128)(2,1)} %bitcast.245, bf16[3,65536]{1,0:T(4,128)(2,1)} %bitcast.247, bf16[3,65536]{1,0:T(4,128)(2,1)} %bitcast.246), kind=kOutput, calls=%fused_computation.1.clone.1 | convolution fusion | flops 150732800 | bytes 1968000 | tf_op jit(solution)/shard_map/while/body/eval_jaxpr/dot_general | solution.py:35
  61.0 8.7 %convolution_convert_fusion.3 = bf16[65536,6]{0,1:T(8,128)(2,1)S(1)} fusion(bf16[6,64]{1,0:T(8,128)(2,1)S(1)} %get-tuple-element.295, bf16[9,64]{1,0:T(8,128)(2,1)S(1)} %get-tuple-element.294, bf16[3,65536]{1,0:T(4,128)(2,1)} %bitcast.245, bf16[3,65536]{1,0:T(4,128)(2,1)} %bitcast.247, bf16[3,65536]{1,0:T(4,128)(2,1)} %bitcast.246), kind=kOutput, calls=%fused_computation.1.clone.1 | convolution fusion | flops 150732800 | bytes 1968000 | tf_op jit(solution)/shard_map/while/body/eval_jaxpr/dot_general | solution.py:35
  138.9 31.2 %collective-permute-done.2 = bf16[3,3,128,512]{3,2,1,0:T(8,128)(2,1)} collective-permute-done((bf16[3,3,128,512]{3,2,1,0:T(8,128)(2,1)}, bf16[3,3,128,512]{3,2,1,0:T(8,128)(2,1)}, u32[]{:S(2)}, u32[]{:S(2)}) %collective-permute-start.2) | collective-permute-done | bytes 1179680 | tf_op jit(solution)/shard_map/ppermute | solution.py:19
  170.1 23.8 %collective-permute-done.3 = bf16[3,3,128,512]{3,2,1,0:T(8,128)(2,1)} collective-permute-done((bf16[3,3,128,512]{3,2,1,0:T(8,128)(2,1)}, bf16[3,3,128,512]{3,2,1,0:T(8,128)(2,1)}, u32[]{:S(2)}, u32[]{:S(2)}) %collective-permute-start.3) | collective-permute-done | bytes 1179680 | tf_op jit(solution)/shard_map/ppermute | solution.py:21
  212.6 18.6 %subtract_convert_fusion = (bf16[3,4,128,512]{3,2,1,0:T(8,128)(2,1)}, bf16[3,4,128,512]{3,2,1,0:T(8,128)(2,1)}) fusion(bf16[3,4,128,512]{3,2,1,0:T(8,128)(2,1)} %param.12, f32[3,10,128,512]{3,2,1,0:T(8,128)} %maximum_convert_fusion.1, f32[4,128,512]{2,1,0:T(8,128)} %get-tuple-element.157, f32[3,10,128,512]{3,2,1,0:T(8,128)} %maximum_convert_fusion, ...), kind=kOutput, calls=%fused_computation.79 | convolution fusion | flops 829685760 | bytes 54526464 | tf_op jit(solution)/shard_map/dot_general | solution.py:110
  245.5 13.6 %all-to-all-done.3 = bf16[3,4,128,512]{2,1,0,3:T(4,128)(2,1)} async-done(((bf16[3,4,128,512]{2,1,0,3:T(4,128)(2,1)}), bf16[3,4,128,512]{2,1,0,3:T(4,128)(2,1)}, u32[]{:S(2)}, u32[]{:S(2)}) %all-to-all-start.3) | async-done | bytes 1572896 | tf_op jit(solution)/shard_map/all_to_all | solution.py:125
  281.3 14.6 %collective-permute-done.5 = bf16[3,3,128,512]{3,2,1,0:T(8,128)(2,1)} collective-permute-done((bf16[3,3,128,512]{3,2,1,0:T(8,128)(2,1)}, bf16[3,3,128,512]{3,2,1,0:T(8,128)(2,1)}, u32[]{:S(2)}, u32[]{:S(2)}) %collective-permute-start.5) | collective-permute-done | bytes 1179680 | tf_op jit(solution)/shard_map/ppermute | solution.py:21
  323.3 142.0 %while.24 = (s32[]{:T(128)}, f32[9,64]{1,0:T(8,128)S(1)}, f32[6,64]{1,0:T(8,128)S(1)}, bf16[4,3,1,128,512]{4,3,2,1,0:T(8,128)(2,1)}, bf16[4,6,1,128,512]{4,3,0,2...) while((s32[]{:T(128)}, f32[9,64]{1,0:T(8,128)S(1)}, ...), condition=%wide.region_3.4_spmd.clone, body=%wide.region_2.3_spmd.clone.sunk | while | flops 319031168 | bytes 64103916 | solution.py:160
  326.1 8.2 %convolution_bitcast_fusion.4 = f32[64,65536]{1,0:T(8,128)} fusion(bf16[9,64]{1,0:T(8,128)(2,1)S(1)} %get-tuple-element.321, bf16[3,65536]{1,0:T(4,128)(2,1)S(1)} %bitcast.236, bf16[3,65536]{1,0:T(4,128)(2,1)S(1)} %bitcast.240, bf16[3,65536]{1,0:T(4,128)(2,1)S(1)} %bitcast.238), kind=kOutput, calls=%fused_computation.16.clone.1 | convolution fusion | flops 79036416 | bytes 17958016 | tf_op jit(solution)/shard_map/while/body/eval_jaxpr/dot_general | solution.py:39
  335.9 8.1 %fusion.121 = f32[6,64]{1,0:T(8,128)S(1)} fusion(bf16[6,65536]{1,0:T(8,128)(2,1)S(1)} %bitcast.242, f32[64,65536]{1,0:T(8,128)} %convolution_bitcast_fusion.4, f32[6,64]{1,0:T(8,128)S(1)} %get-tuple-element.308, pred[]{:T(512)S(6)} %compare.3), kind=kOutput, calls=%fused_computation.27.clone.1 | convolution fusion | flops 71303936 | bytes 17566720 | tf_op jit(solution)/shard_map/while/body/eval_jaxpr/dot_general | solution.py:42
  344.0 14.9 %fusion.120 = f32[9,64]{1,0:T(8,128)S(1)} fusion(bf16[6,65536]{1,0:T(8,128)(2,1)S(1)} %bitcast.243, bf16[6,64]{1,0:T(8,128)(2,1)S(1)} %get-tuple-element.320, f32[64,65536]{1,0:T(8,128)} %convolution_bitcast_fusion.4, bf16[3,65536]{1,0:T(4,128)(2,1)S(1)} %bitcast.237, bf16[3,65536]{1,0:T(4,128)(2,1)S(1)} %bitcast.241, ...), kind=kOutput, calls=%fused_computation.26.clone.1 | convolution fusion | flops 167117952 | bytes 18748672 | tf_op jit(solution)/shard_map/while/body/eval_jaxpr/dot_general | solution.py:49
  361.6 8.2 %convolution_bitcast_fusion.4 = f32[64,65536]{1,0:T(8,128)} fusion(bf16[9,64]{1,0:T(8,128)(2,1)S(1)} %get-tuple-element.321, bf16[3,65536]{1,0:T(4,128)(2,1)S(1)} %bitcast.236, bf16[3,65536]{1,0:T(4,128)(2,1)S(1)} %bitcast.240, bf16[3,65536]{1,0:T(4,128)(2,1)S(1)} %bitcast.238), kind=kOutput, calls=%fused_computation.16.clone.1 | convolution fusion | flops 79036416 | bytes 17958016 | tf_op jit(solution)/shard_map/while/body/eval_jaxpr/dot_general | solution.py:39
  371.4 8.1 %fusion.121 = f32[6,64]{1,0:T(8,128)S(1)} fusion(bf16[6,65536]{1,0:T(8,128)(2,1)S(1)} %bitcast.242, f32[64,65536]{1,0:T(8,128)} %convolution_bitcast_fusion.4, f32[6,64]{1,0:T(8,128)S(1)} %get-tuple-element.308, pred[]{:T(512)S(6)} %compare.3), kind=kOutput, calls=%fused_computation.27.clone.1 | convolution fusion | flops 71303936 | bytes 17566720 | tf_op jit(solution)/shard_map/while/body/eval_jaxpr/dot_general | solution.py:42
  379.5 14.9 %fusion.120 = f32[9,64]{1,0:T(8,128)S(1)} fusion(bf16[6,65536]{1,0:T(8,128)(2,1)S(1)} %bitcast.243, bf16[6,64]{1,0:T(8,128)(2,1)S(1)} %get-tuple-element.320, f32[64,65536]{1,0:T(8,128)} %convolution_bitcast_fusion.4, bf16[3,65536]{1,0:T(4,128)(2,1)S(1)} %bitcast.237, bf16[3,65536]{1,0:T(4,128)(2,1)S(1)} %bitcast.241, ...), kind=kOutput, calls=%fused_computation.26.clone.1 | convolution fusion | flops 167117952 | bytes 18748672 | tf_op jit(solution)/shard_map/while/body/eval_jaxpr/dot_general | solution.py:49
  397.1 8.2 %convolution_bitcast_fusion.4 = f32[64,65536]{1,0:T(8,128)} fusion(bf16[9,64]{1,0:T(8,128)(2,1)S(1)} %get-tuple-element.321, bf16[3,65536]{1,0:T(4,128)(2,1)S(1)} %bitcast.236, bf16[3,65536]{1,0:T(4,128)(2,1)S(1)} %bitcast.240, bf16[3,65536]{1,0:T(4,128)(2,1)S(1)} %bitcast.238), kind=kOutput, calls=%fused_computation.16.clone.1 | convolution fusion | flops 79036416 | bytes 17958016 | tf_op jit(solution)/shard_map/while/body/eval_jaxpr/dot_general | solution.py:39
  406.9 8.1 %fusion.121 = f32[6,64]{1,0:T(8,128)S(1)} fusion(bf16[6,65536]{1,0:T(8,128)(2,1)S(1)} %bitcast.242, f32[64,65536]{1,0:T(8,128)} %convolution_bitcast_fusion.4, f32[6,64]{1,0:T(8,128)S(1)} %get-tuple-element.308, pred[]{:T(512)S(6)} %compare.3), kind=kOutput, calls=%fused_computation.27.clone.1 | convolution fusion | flops 71303936 | bytes 17566720 | tf_op jit(solution)/shard_map/while/body/eval_jaxpr/dot_general | solution.py:42
  415.0 14.9 %fusion.120 = f32[9,64]{1,0:T(8,128)S(1)} fusion(bf16[6,65536]{1,0:T(8,128)(2,1)S(1)} %bitcast.243, bf16[6,64]{1,0:T(8,128)(2,1)S(1)} %get-tuple-element.320, f32[64,65536]{1,0:T(8,128)} %convolution_bitcast_fusion.4, bf16[3,65536]{1,0:T(4,128)(2,1)S(1)} %bitcast.237, bf16[3,65536]{1,0:T(4,128)(2,1)S(1)} %bitcast.241, ...), kind=kOutput, calls=%fused_computation.26.clone.1 | convolution fusion | flops 167117952 | bytes 18748672 | tf_op jit(solution)/shard_map/while/body/eval_jaxpr/dot_general | solution.py:49
  432.5 8.2 %convolution_bitcast_fusion.4 = f32[64,65536]{1,0:T(8,128)} fusion(bf16[9,64]{1,0:T(8,128)(2,1)S(1)} %get-tuple-element.321, bf16[3,65536]{1,0:T(4,128)(2,1)S(1)} %bitcast.236, bf16[3,65536]{1,0:T(4,128)(2,1)S(1)} %bitcast.240, bf16[3,65536]{1,0:T(4,128)(2,1)S(1)} %bitcast.238), kind=kOutput, calls=%fused_computation.16.clone.1 | convolution fusion | flops 79036416 | bytes 17958016 | tf_op jit(solution)/shard_map/while/body/eval_jaxpr/dot_general | solution.py:39
  442.4 8.1 %fusion.121 = f32[6,64]{1,0:T(8,128)S(1)} fusion(bf16[6,65536]{1,0:T(8,128)(2,1)S(1)} %bitcast.242, f32[64,65536]{1,0:T(8,128)} %convolution_bitcast_fusion.4, f32[6,64]{1,0:T(8,128)S(1)} %get-tuple-element.308, pred[]{:T(512)S(6)} %compare.3), kind=kOutput, calls=%fused_computation.27.clone.1 | convolution fusion | flops 71303936 | bytes 17566720 | tf_op jit(solution)/shard_map/while/body/eval_jaxpr/dot_general | solution.py:42
  450.4 14.9 %fusion.120 = f32[9,64]{1,0:T(8,128)S(1)} fusion(bf16[6,65536]{1,0:T(8,128)(2,1)S(1)} %bitcast.243, bf16[6,64]{1,0:T(8,128)(2,1)S(1)} %get-tuple-element.320, f32[64,65536]{1,0:T(8,128)} %convolution_bitcast_fusion.4, bf16[3,65536]{1,0:T(4,128)(2,1)S(1)} %bitcast.237, bf16[3,65536]{1,0:T(4,128)(2,1)S(1)} %bitcast.241, ...), kind=kOutput, calls=%fused_computation.26.clone.1 | convolution fusion | flops 167117952 | bytes 18748672 | tf_op jit(solution)/shard_map/while/body/eval_jaxpr/dot_general | solution.py:49
  465.4 76.3 %all-reduce = (f32[9,64]{1,0:T(8,128)}, f32[6,64]{1,0:T(8,128)}) all-reduce(f32[9,64]{1,0:T(8,128)S(1)} %get-tuple-element.69, f32[6,64]{1,0:T(8,128)S(1)} %get-tuple-element.70), channel_id=1, replica_groups=mesh['rep'=2,'row'=4,'col'=4] {'row','col'}, use_global_device_ids=true, to_apply=%region_4.5 | all-reduce | flops 960 | bytes 7680 | tf_op jit(solution)/shard_map/psum | solution.py:161
  (181 shorter events, 202.7 us)
Async XLA Ops:
  0.6 134.5 %copy-start = (bf16[512,512]{1,0:T(8,128)(2,1)S(1)}, bf16[512,512]{1,0:T(8,128)(2,1)}, u32[]{:S(2)}) copy-start(bf16[512,512]{1,0:T(8,128)(2,1)} %param.15) | copy-start | bytes 1572868
  0.6 9.3 %copy-start.2 = (bf16[3,4,128,512]{3,2,1,0:T(8,128)(2,1)S(1)}, bf16[3,4,128,512]{3,2,1,0:T(8,128)(2,1)}, u32[]{:S(2)}) copy-start(bf16[3,4,128,512]{3,2,1,0:T(8,128)(2,1)} %param.11) | copy-start | bytes 4718596
  4.6 6.7 %copy-start.19 = (bf16[9,64]{1,0:T(8,128)(2,1)S(1)}, bf16[9,64]{1,0:T(8,128)(2,1)}, u32[]{:S(2)}) copy-start(bf16[9,64]{1,0:T(8,128)(2,1)} %param.13) | copy-start | bytes 3460
  4.6 6.7 %copy-start.20 = (bf16[6,64]{1,0:T(8,128)(2,1)S(1)}, bf16[6,64]{1,0:T(8,128)(2,1)}, u32[]{:S(2)}) copy-start(bf16[6,64]{1,0:T(8,128)(2,1)} %param.14) | copy-start | bytes 2308
  4.6 75.7 %all-to-all-start.1 = ((bf16[3,4,128,512]{2,1,0,3:T(4,128)(2,1)}), bf16[3,4,128,512]{2,1,0,3:T(4,128)(2,1)}, u32[]{:S(2)}, u32[]{:S(2)}) async-start(bf16[3,4,128,512]{2,1,0,3:T(4,128)(2,1)} %copy.22), calls=%async_computation.1 | async-start | bytes 3145728 | tf_op jit(solution)/shard_map/all_to_all | solution.py:86
  80.4 32.4 %all-to-all-start = ((bf16[3,4,128,512]{2,1,0,3:T(4,128)(2,1)}), bf16[3,4,128,512]{2,1,0,3:T(4,128)(2,1)}, u32[]{:S(2)}, u32[]{:S(2)}) async-start(bf16[3,4,128,512]{2,1,0,3:T(4,128)(2,1)} %copy.20), calls=%async_computation | async-start | bytes 3145728 | tf_op jit(solution)/shard_map/all_to_all | solution.py:103
  88.1 110.4 %collective-permute-start = (bf16[3,3,128,512]{3,2,1,0:T(8,128)(2,1)}, bf16[3,3,128,512]{3,2,1,0:T(8,128)(2,1)}, u32[]{:S(2)}, u32[]{:S(2)}) collective-permute-start(bf16[3,3,128,512]{3,2,1,0:T(8,128)(2,1)} %get-tuple-element.166), channel_id=1, source_target_pairs={{0,1},{1,2},{2,3},{3,0},{4,5},{5,6},{6,7},{7,4},{8,9},{9,10},{10,1... | collective-permute-start | bytes 3538952 | tf_op jit(solution)/shard_map/ppermute | solution.py:19
  90.3 108.2 %collective-permute-start.1 = (bf16[3,3,128,512]{3,2,1,0:T(8,128)(2,1)}, bf16[3,3,128,512]{3,2,1,0:T(8,128)(2,1)}, u32[]{:S(2)}, u32[]{:S(2)}) collective-permute-start(bf16[3,3,128,512]{3,2,1,0:T(8,128)(2,1)} %get-tuple-element.167), channel_id=1, source_target_pairs={{1,0},{2,1},{3,2},{0,3},{5,4},{6,5},{7,6},{4,7},{9,8},{10,9},{11,1... | collective-permute-start | bytes 3538952 | tf_op jit(solution)/shard_map/ppermute | solution.py:21
  94.0 6.1 %copy-start.21 = (f32[16]{0:T(128)S(1)}, f32[16]{0:T(128)}, u32[]{:S(2)}) copy-start(f32[16]{0:T(128)} %param.17) | copy-start | bytes 196
  94.0 76.1 %collective-permute-start.2 = (bf16[3,3,128,512]{3,2,1,0:T(8,128)(2,1)}, bf16[3,3,128,512]{3,2,1,0:T(8,128)(2,1)}, u32[]{:S(2)}, u32[]{:S(2)}) collective-permute-start(bf16[3,3,128,512]{3,2,1,0:T(8,128)(2,1)} %get-tuple-element.168), channel_id=1, source_target_pairs={{0,1},{1,2},{2,3},{3,0},{4,5},{5,6},{6,7},{7,4},{8,9},{9,10},{10,1... | collective-permute-start | bytes 3538952 | tf_op jit(solution)/shard_map/ppermute | solution.py:19
  94.0 99.9 %collective-permute-start.3 = (bf16[3,3,128,512]{3,2,1,0:T(8,128)(2,1)}, bf16[3,3,128,512]{3,2,1,0:T(8,128)(2,1)}, u32[]{:S(2)}, u32[]{:S(2)}) collective-permute-start(bf16[3,3,128,512]{3,2,1,0:T(8,128)(2,1)} %get-tuple-element.169), channel_id=1, source_target_pairs={{1,0},{2,1},{3,2},{0,3},{5,4},{6,5},{7,6},{4,7},{9,8},{10,9},{11,1... | collective-permute-start | bytes 3538952 | tf_op jit(solution)/shard_map/ppermute | solution.py:21
  126.8 8.3 %copy-start.12 = (bf16[1,4,128,512]{3,2,1,0:T(8,128)(2,1)S(1)}, bf16[1,4,128,512]{3,2,1,0:T(8,128)(2,1)}, u32[]{:S(2)}) copy-start(bf16[1,4,128,512]{3,2,1,0:T(8,128)(2,1)} %copy-done.11) | copy-start | bytes 1572868
  126.8 8.3 %copy-start.17 = (bf16[1,4,128,512]{3,2,1,0:T(8,128)(2,1)S(1)}, bf16[1,4,128,512]{3,2,1,0:T(8,128)(2,1)}, u32[]{:S(2)}) copy-start(bf16[1,4,128,512]{3,2,1,0:T(8,128)(2,1)} %copy-done.16) | copy-start | bytes 1572868
  130.7 72.5 %all-to-all-start.2 = ((bf16[3,4,512,128]{3,1,0,2:T(4,128)(2,1)}), bf16[3,4,512,128]{3,1,0,2:T(4,128)(2,1)}, u32[]{:S(2)}, u32[]{:S(2)}) async-start(bf16[3,4,512,128]{3,1,0,2:T(4,128)(2,1)} %copy.24), calls=%async_computation.2 | async-start | bytes 3145728 | tf_op jit(solution)/shard_map/all_to_all | solution.py:117
  138.9 59.6 %copy-start.8 = (bf16[1,4,128,512]{3,2,1,0:T(8,128)(2,1)S(1)}, bf16[1,4,128,512]{3,2,1,0:T(8,128)(2,1)}, u32[]{:S(2)}) copy-start(bf16[1,4,128,512]{3,2,1,0:T(8,128)(2,1)} %copy-done.7) | copy-start | bytes 1572868
  138.9 59.6 %copy-start.10 = (bf16[1,4,128,512]{3,2,1,0:T(8,128)(2,1)S(1)}, bf16[1,4,128,512]{3,2,1,0:T(8,128)(2,1)}, u32[]{:S(2)}) copy-start(bf16[1,4,128,512]{3,2,1,0:T(8,128)(2,1)} %copy-done.9) | copy-start | bytes 1572868
  207.5 5.1 copy-start.18
  231.2 8.7 %copy-start.3 = (bf16[3,4,128,512]{3,2,1,0:T(8,128)(2,1)S(1)}, bf16[3,4,128,512]{3,2,1,0:T(8,128)(2,1)}, u32[]{:S(2)}) copy-start(bf16[3,4,128,512]{3,2,1,0:T(8,128)(2,1)} %get-tuple-element.154) | copy-start | bytes 4718596
  235.2 24.0 %all-to-all-start.3 = ((bf16[3,4,128,512]{2,1,0,3:T(4,128)(2,1)}), bf16[3,4,128,512]{2,1,0,3:T(4,128)(2,1)}, u32[]{:S(2)}, u32[]{:S(2)}) async-start(bf16[3,4,128,512]{2,1,0,3:T(4,128)(2,1)} %copy.26), calls=%async_computation.3 | async-start | bytes 3145728 | tf_op jit(solution)/shard_map/all_to_all | solution.py:125
  241.6 38.8 %collective-permute-start.4 = (bf16[3,3,128,512]{3,2,1,0:T(8,128)(2,1)}, bf16[3,3,128,512]{3,2,1,0:T(8,128)(2,1)}, u32[]{:S(2)}, u32[]{:S(2)}) collective-permute-start(bf16[3,3,128,512]{3,2,1,0:T(8,128)(2,1)} %get-tuple-element.164), channel_id=1, source_target_pairs={{0,1},{1,2},{2,3},{3,0},{4,5},{5,6},{6,7},{7,4},{8,9},{9,10},{10,1... | collective-permute-start | bytes 3538952 | tf_op jit(solution)/shard_map/ppermute | solution.py:19
  242.7 53.2 %collective-permute-start.5 = (bf16[3,3,128,512]{3,2,1,0:T(8,128)(2,1)}, bf16[3,3,128,512]{3,2,1,0:T(8,128)(2,1)}, u32[]{:S(2)}, u32[]{:S(2)}) collective-permute-start(bf16[3,3,128,512]{3,2,1,0:T(8,128)(2,1)} %get-tuple-element.165), channel_id=1, source_target_pairs={{1,0},{2,1},{3,2},{0,3},{5,4},{6,5},{7,6},{4,7},{9,8},{10,9},{11,1... | collective-permute-start | bytes 3538952 | tf_op jit(solution)/shard_map/ppermute | solution.py:21
  259.1 7.5 %copy-start.15 = (bf16[512,512]{1,0:T(8,128)(2,1)S(1)}, bf16[512,512]{1,0:T(8,128)(2,1)}, u32[]{:S(2)}) copy-start(bf16[512,512]{1,0:T(8,128)(2,1)} %param.16) | copy-start | bytes 1572868
  273.9 27.8 %all-to-all-start.4 = ((bf16[3,4,512,128]{3,1,0,2:T(4,128)(2,1)}), bf16[3,4,512,128]{3,1,0,2:T(4,128)(2,1)}, u32[]{:S(2)}, u32[]{:S(2)}) async-start(bf16[3,4,512,128]{3,1,0,2:T(4,128)(2,1)} %copy.28), calls=%async_computation.4 | async-start | bytes 3145728 | tf_op jit(solution)/shard_map/all_to_all | solution.py:128
  465.3 76.3 %copy-start.1 = (bf16[512,512]{1,0:T(8,128)(2,1)S(1)}, bf16[512,512]{1,0:T(8,128)(2,1)}, u32[]{:S(2)}) copy-start(bf16[512,512]{1,0:T(8,128)(2,1)} %param.15) | copy-start | bytes 1572868
  (9 other events, 24.1 us)
where the time goes:
time: 552 us; the launch traced here: 542 us
  matrix products  191 us (35%)
  local copies, waits for them, and re-layouts  120 us (22%)
  waiting for transfers between devices  83.2 us (15%)
  blocking collectives  76.3 us (14%)
  starting transfers between devices  35.2 us (6%)
  other arithmetic  34.7 us (6%)
    psum x1, blocking collectives, local(): grad_w_in, grad_w_out = lax.psum((totals[0], totals[1]), ('row', 'col'))  76.3 us
    dot_general x4, matrix products, closure_backward(): lax.dot_general(features, back_pre, (((1,), (1,)), ((), ())), preferred_e...  59.6 us
    ppermute x3, waiting for transfers between devices, padded_2(): lax.ppermute(head, axis, [((i + 1) % count, i) for i in range(count)])  38.4 us
    dot_general x4, matrix products, closure_forward(): jnp.dot(w_out, hidden, preferred_element_type=jnp.float32)  34.8 us
    dot_general x4, matrix products, closure_backward(): preact = jnp.dot(w_in.T, features, preferred_element_type=jnp.float32)  32.7 us
    while x40, local copies, waits for them, and re-layouts  32.6 us
    dot_general x4, matrix products, closure_backward(): lax.dot_general(upstream, hidden, (((1,), (1,)), ((), ())), preferred_ele...  32.3 us
    ppermute x3, waiting for transfers between devices, padded_2(): lax.ppermute(tail, axis, [(i, (i + 1) % count) for i in range(count)])  31.2 us
  transfers between devices with their start and end apart: 11, of which 4 were waited for; matrix products, arithmetic and copies ran while one was open for 25% of the time, Pallas kernels for 0%

commit v1 on v0

v1 whole, which is shorter than its diff:
```python
import functools
import math

import jax
import jax.numpy as jnp
from jax import lax
from jax.experimental import pallas as pl
from jax.experimental.pallas import tpu as pltpu
from jax.sharding import PartitionSpec as P

COEFS = (0.75, -0.15, 1.0 / 60.0)
STEP_SIZE = 0.3
ROWS = 16
XX, YY, ZZ, XY, XZ, YZ = range(6)
F32, BF16 = jnp.float32, jnp.bfloat16
MESH = pl.DeviceIdType.MESH


def dot(a, b):
    return jnp.dot(a, b, preferred_element_type=F32)


def dot_nt(a, b):
    return lax.dot_general(a, b, (((1,), (1,)), ((), ())), preferred_element_type=F32)


def features_of(parts):
    wide = [p.astype(F32) for p in parts]
    n = wide[0].shape[1]
    left = [pltpu.roll(w, 1, 1).astype(BF16) for w in wide]
    right = [pltpu.roll(w, n - 1, 1).astype(BF16) for w in wide]
    return jnp.concatenate(left + list(parts) + right, 0)


def forward_kernel(nat, chunked, v_ref, win_ref, wout_ref, *outs):
    y_cells = v_ref.shape[2]
    total_rows, quarter = win_ref.shape[0], win_ref.shape[0] // 4

    def body(g, carry):
        rows = pl.ds(pl.multiple_of(g * ROWS, ROWS), ROWS)
        feats = features_of([v_ref[c, 0, rows, :] for c in range(3)])
        stress = None
        for q in range(4):
            part = slice(q * quarter, (q + 1) * quarter)
            half = dot(win_ref[part, :], feats)
            hidden = (half + half * jnp.tanh(half)).astype(BF16)
            term = dot(wout_ref[:, part], hidden)
            stress = term if stress is None else stress + term
        stress = stress.astype(BF16)
        for i, k in enumerate(nat):
            outs[0][i, 0, rows, :] = stress[k * ROWS : (k + 1) * ROWS]
        if chunked:
            count, width = outs[1].shape[0], outs[1].shape[4]
            for i, k in enumerate(chunked):
                for d in range(count):
                    outs[1][d, i, 0, rows, :] = stress[
                        k * ROWS : (k + 1) * ROWS, d * width : (d + 1) * width
                    ]
        return carry

    lax.fori_loop(0, y_cells // ROWS, body, 0)


def closure_forward(v, win, wout, nat, chunked, count):
    _, z, y, x = v.shape
    out_shape = [jax.ShapeDtypeStruct((len(nat), z, y, x), BF16)]
    out_specs = [pl.BlockSpec((len(nat), 1, y, x), lambda i: (0, i, 0, 0))]
    if chunked:
        n, w = len(chunked), x // count
        out_shape.append(jax.ShapeDtypeStruct((count, n, z, y, w), BF16))
        out_specs.append(pl.BlockSpec((count, n, 1, y, w), lambda i: (0, 0, i, 0, 0)))
    cells = z * y * x
    return pl.pallas_call(
        functools.partial(forward_kernel, nat, chunked),
        grid=(z,),
        out_shape=out_shape,
        in_specs=[
            pl.BlockSpec((3, 1, y, x), lambda i: (0, i, 0, 0)),
            pl.BlockSpec(win.shape, lambda i: (0, 0)),
            pl.BlockSpec(wout.shape, lambda i: (0, 0)),
        ],
        out_specs=out_specs,
        cost_estimate=pl.CostEstimate(
            flops=cells * 64 * 300, bytes_accessed=cells * 20, transcendentals=cells * 64
        ),
        name="closure_forward",
    )(v, win, wout)


def pencil_kernel(dy_ref, s_ref, v_ref, o_ref):
    r, _, _, yl, w = s_ref.shape
    n = r * yl
    v1 = v_ref[:, 1, 0].reshape(n, w).astype(F32)
    for c in range(3):
        both = jnp.concatenate([s_ref[:, c, 0].reshape(n, w), v_ref[:, c, 0].reshape(n, w)], 1)
        out = dot(dy_ref[...], both)
        o_ref[:, c, 0] = (out[:, :w] + v1 * out[:, w:]).astype(BF16).reshape(r, yl, w)


def pencil_adj_kernel(dy_ref, q_ref, o_ref):
    r, _, _, yl, w = q_ref.shape
    n = r * yl
    both = jnp.concatenate([q_ref[:, c, 0].reshape(n, w) for c in range(3)], 1)
    out = dot(dy_ref[...], both).astype(BF16)
    for c in range(3):
        o_ref[:, c, 0] = out[:, c * w : (c + 1) * w].reshape(r, yl, w)


def pencil_call(kernel, matrix, *fields):
    r, n, z, yl, w = fields[0].shape
    spec = pl.BlockSpec((r, n, 1, yl, w), lambda i: (0, 0, i, 0, 0))
    return pl.pallas_call(
        kernel,
        grid=(z,),
        out_shape=jax.ShapeDtypeStruct(fields[0].shape, BF16),
        in_specs=[pl.BlockSpec(matrix.shape, lambda i: (0, 0))] + [spec] * len(fields),
        out_specs=spec,
        name="pencil",
    )(matrix, *fields)


def stencil(planes, k):
    total = None
    for reach in (1, 2, 3):
        term = COEFS[reach - 1] * (planes[k + 3 + reach] - planes[k + 3 - reach])
        total = term if total is None else total + term
    return total


def advance_kernel(
    metric_ref, v_ref, lo_ref, hi_ref, t_ref, s_ref, slo_ref, shi_ref, py_ref, dxt_ref,
    new_ref, res_ref, chunk_ref,
):
    _, z, yb, x = v_ref.shape
    count, w = chunk_ref.shape[0], chunk_ref.shape[4]
    for c in range(3):
        lhs = jnp.concatenate(
            [s_ref[c].reshape(z * yb, x), v_ref[c].reshape(z * yb, x)], 0
        )
        out = dot(lhs, dxt_ref[...])
        v_planes = [lo_ref[c, k].astype(F32) for k in range(3)]
        v_planes += [v_ref[c, k].astype(F32) for k in range(z)]
        v_planes += [hi_ref[c, k].astype(F32) for k in range(3)]
        s_planes = [slo_ref[c, k].astype(F32) for k in range(3)]
        s_planes += [s_ref[2 + c, k].astype(F32) for k in range(z)]
        s_planes += [shi_ref[c, k].astype(F32) for k in range(3)]
        for k in range(z):
            v0 = v_ref[0, k].astype(F32)
            v2 = v_ref[2, k].astype(F32)
            part_x = out[k * yb : (k + 1) * yb] + v0 * out[(z + k) * yb : (z + k + 1) * yb]
            part_z = metric_ref[k + 3] * (stencil(s_planes, k) + v2 * stencil(v_planes, k))
            part_y = jnp.concatenate([py_ref[d, c, k] for d in range(count)], 1).astype(F32)
            advanced = v_planes[k + 3] - STEP_SIZE * (part_x + part_y + part_z)
            new_ref[c, k] = advanced.astype(BF16)
            res = (advanced - t_ref[c, k].astype(F32)).astype(BF16)
            res_ref[c, k] = res
            for d in range(count):
                chunk_ref[d, c, k] = res[:, d * w : (d + 1) * w]


def backward_kernel(
    scale, metric_ref, v_ref, r_ref, rlo_ref, rhi_ref, ay_ref, dx_ref, win_ref, wot_ref,
    o_ref, gin_ref, gout_ref, up_ref,
):
    _, z, yb, x = v_ref.shape
    count = ay_ref.shape[0]
    step = pl.program_id(0)

    @pl.when(step == 0)
    def _():
        gin_ref[...] = jnp.zeros_like(gin_ref)
        gout_ref[...] = jnp.zeros_like(gout_ref)

    adj_x = dot(r_ref[...].reshape(3 * z * yb, x), dx_ref[...])
    weighted = []
    for c in range(3):
        planes = [rlo_ref[c, k].astype(F32) * metric_ref[k] for k in range(3)]
        planes += [r_ref[c, k].astype(F32) * metric_ref[k + 3] for k in range(z)]
        planes += [rhi_ref[c, k].astype(F32) * metric_ref[k + 3 + z] for k in range(3)]
        weighted.append(planes)
    for k in range(z):
        ax = [adj_x[(c * z + k) * yb : (c * z + k + 1) * yb] for c in range(3)]
        ay = [
            jnp.concatenate([ay_ref[d, c, k] for d in range(count)], 1).astype(F32)
            for c in range(3)
        ]
        az = [-stencil(weighted[c], k) for c in range(3)]
        six = [ax[0], ay[1], az[2], ax[1] + ay[0], ax[2] + az[0], ay[2] + az[1]]
        for i in range(6):
            up_ref[k, i * yb : (i + 1) * yb, :] = (scale * six[i]).astype(BF16)

    quarter = win_ref.shape[0] // 4

    def body(k, carry):
        feats = features_of([v_ref[c, k] for c in range(3)])
        up = up_ref[k]
        for q in range(4):
            part = slice(q * quarter, (q + 1) * quarter)
            half = dot(win_ref[part, :], feats)
            t = jnp.tanh(half)
            one = 1.0 + t
            hidden = (half * one).astype(BF16)
            back_hidden = dot(wot_ref[part, :], up)
            back = (back_hidden * (one * (1.0 + half * (1.0 - t)))).astype(BF16)
            gout_ref[:, part] += dot_nt(up, hidden)
            gin_ref[:, part] += dot_nt(feats, back)
        return carry

    lax.fori_loop(0, z, body, 0)

    @pl.when(step == pl.num_programs(0) - 1)
    def _():
        total_cols = gin_ref.shape[1]
        ch = total_cols // ROWS

        def collapse(ref, offset):
            rows = ref.shape[0]
            row = lax.broadcasted_iota(jnp.int32, (rows, total_cols), 0)
            col = lax.broadcasted_iota(jnp.int32, (rows, total_cols), 1)
            kept = jnp.where(row % ROWS == col // ch, ref[...], 0.0)
            pick_r = (
                lax.broadcasted_iota(jnp.int32, (16, rows), 0)
                == lax.broadcasted_iota(jnp.int32, (16, rows), 1) // ROWS + offset
            ).astype(F32)
            pick_c = (
                lax.broadcasted_iota(jnp.int32, (total_cols, ch), 0) % ch
                == lax.broadcasted_iota(jnp.int32, (total_cols, ch), 1)
            ).astype(F32)
            first = jnp.dot(
                pick_r, kept, preferred_element_type=F32, precision=lax.Precision.HIGHEST
            )
            return jnp.dot(
                first, pick_c, preferred_element_type=F32, precision=lax.Precision.HIGHEST
            )

        o_ref[...] = collapse(gin_ref, 0) + collapse(gout_ref, 9)


def reduce_kernel(sizes, x_ref, o_ref, slots, mid, send_sems, recv_sems):
    axes = tuple(sizes)
    barrier = pltpu.get_barrier_semaphore()
    greeted = 0
    for axis in axes:
        n = sizes[axis]
        me = lax.axis_index(axis)
        for d in range(1, n):
            peer = lax.rem(me + d, n)
            pl.semaphore_signal(barrier, inc=1, device_id={axis: peer}, device_id_type=MESH)
            greeted += 1
    pl.semaphore_wait(barrier, greeted)
    for a, axis in enumerate(axes):
        n = sizes[axis]
        me = lax.axis_index(axis)
        src = x_ref if a == 0 else mid
        copies = []
        for d in range(1, n):
            peer = lax.rem(me + d, n)
            copy = pltpu.make_async_remote_copy(
                src_ref=src,
                dst_ref=slots.at[a, me],
                send_sem=send_sems.at[a, d],
                recv_sem=recv_sems.at[a, d],
                device_id={axis: peer},
                device_id_type=MESH,
            )
            copy.start()
            copies.append(copy)
        slots[a, pl.ds(me, 1)] = src[...][None]
        for copy in copies:
            copy.wait()
        total = slots[a, 0]
        for i in range(1, n):
            total = total + slots[a, i]
        if a == len(axes) - 1:
            o_ref[...] = total
        else:
            mid[...] = total


def reduce_all(g, sizes):
    most = max(sizes.values())
    return pl.pallas_call(
        functools.partial(reduce_kernel, sizes),
        out_shape=jax.ShapeDtypeStruct(g.shape, F32),
        in_specs=[pl.BlockSpec(memory_space=pltpu.VMEM)],
        out_specs=pl.BlockSpec(memory_space=pltpu.VMEM),
        scratch_shapes=[
            pltpu.VMEM((len(sizes), most) + g.shape, F32),
            pltpu.VMEM(g.shape, F32),
            pltpu.SemaphoreType.DMA((len(sizes), most)),
            pltpu.SemaphoreType.DMA((len(sizes), most)),
        ],
        compiler_params=pltpu.CompilerParams(collective_id=0, has_side_effects=True),
        name="reduce_all",
    )(g)


def shift(field, axis, count, up):
    pairs = [(i, (i + 1) % count) for i in range(count)]
    if not up:
        pairs = [(b, a) for a, b in pairs]
    return lax.ppermute(field, axis, pairs)


def halo(field, count):
    n = field.shape[1]
    low = shift(field[:, n - 3 :], "col", count, True)
    high = shift(field[:, :3], "col", count, False)
    return low, high


def swap(chunks):
    return lax.all_to_all(chunks, "row", split_axis=0, concat_axis=0, tiled=True)


def local(sizes, velocity, target, w_in, w_out, diff_x, diff_y, metric_z):
    n_row, n_col = sizes["row"], sizes["col"]
    _, z, y, x = velocity.shape
    y_total, z_total = diff_y.shape[0], metric_z.shape[0]
    ch = w_in.shape[1]
    w = x // n_row
    v_chunks = velocity.reshape(3, z, y, n_row, w).transpose(3, 0, 1, 2, 4)
    v_pencil = swap(v_chunks)
    v_low, v_high = halo(velocity, n_col)

    eye = jnp.eye(ROWS, dtype=BF16)
    half_in = w_in.T * jnp.asarray(0.5, BF16)
    half_out = w_out.T * jnp.asarray(0.5, BF16)
    win = (eye[:, None, None, :] * half_in[None, :, :, None]).reshape(ROWS * ch, 9 * ROWS)
    wout = (eye[None, :, :, None] * w_out[:, None, None, :]).reshape(6 * ROWS, ROWS * ch)
    wot = (eye[:, None, None, :] * half_out[None, :, :, None]).reshape(ROWS * ch, 6 * ROWS)
    wout_z = jnp.concatenate([wout[k * ROWS : (k + 1) * ROWS] for k in (XZ, YZ, ZZ)], 0)

    stress, sy_chunks = closure_forward(
        velocity, win, wout, (XX, XY, XZ, YZ, ZZ), (XY, YY, YZ), n_row
    )
    part_y = swap(pencil_call(pencil_kernel, diff_y, swap(sy_chunks), v_pencil))
    s_low = closure_forward(v_low, win, wout_z, (0, 1, 2), (), 1)[0]
    s_high = closure_forward(v_high, win, wout_z, (0, 1, 2), (), 1)[0]

    start = lax.axis_index("col") * z
    tripled = jnp.concatenate([metric_z, metric_z, metric_z])
    metric = lax.dynamic_slice_in_dim(tripled, start + z_total - 3, z + 6)

    yb = math.gcd(32, y)
    smem = pl.BlockSpec(memory_space=pltpu.SMEM)

    def rows_spec(n, planes, block):
        return pl.BlockSpec((n, planes, block, x), lambda i: (0, 0, i, 0))

    def chunk_spec(block):
        return pl.BlockSpec((n_row, 3, z, block, w), lambda i: (0, 0, 0, i, 0))

    whole_x = pl.BlockSpec((x, x), lambda i: (0, 0))
    new_velocity, residual, res_chunks = pl.pallas_call(
        advance_kernel,
        grid=(y // yb,),
        out_shape=[
            jax.ShapeDtypeStruct(velocity.shape, BF16),
            jax.ShapeDtypeStruct(velocity.shape, BF16),
            jax.ShapeDtypeStruct(v_chunks.shape, BF16),
        ],
        in_specs=[
            smem, rows_spec(3, z, yb), rows_spec(3, 3, yb), rows_spec(3, 3, yb),
            rows_spec(3, z, yb), rows_spec(5, z, yb), rows_spec(3, 3, yb), rows_spec(3, 3, yb),
            chunk_spec(yb), whole_x,
        ],
        out_specs=[rows_spec(3, z, yb), rows_spec(3, z, yb), chunk_spec(yb)],
        name="advance",
    )(metric, velocity, v_low, v_high, target, stress, s_low, s_high, part_y, diff_x.T)

    r_low, r_high = halo(residual, n_col)
    adj_y = swap(pencil_call(pencil_adj_kernel, diff_y.T, swap(res_chunks)))
    scale = -STEP_SIZE / math.sqrt(x * y_total * z_total)
    grads = pl.pallas_call(
        functools.partial(backward_kernel, scale),
        grid=(y // ROWS,),
        out_shape=jax.ShapeDtypeStruct((16, ch), F32),
        in_specs=[
            smem, rows_spec(3, z, ROWS), rows_spec(3, z, ROWS), rows_spec(3, 3, ROWS),
            rows_spec(3, 3, ROWS), chunk_spec(ROWS), whole_x,
            pl.BlockSpec(win.shape, lambda i: (0, 0)),
            pl.BlockSpec(wot.shape, lambda i: (0, 0)),
        ],
        out_specs=pl.BlockSpec((16, ch), lambda i: (0, 0)),
        scratch_shapes=[
            pltpu.VMEM((9 * ROWS, ROWS * ch), F32),
            pltpu.VMEM((6 * ROWS, ROWS * ch), F32),
            pltpu.VMEM((z, 6 * ROWS, x), BF16),
        ],
        name="closure_backward",
    )(metric, velocity, residual, r_low, r_high, adj_y, diff_x, win, wot)
    grads = reduce_all(grads, {"col": n_col, "row": n_row})
    return (new_velocity, grads[:9], grads[9:15])


def solution(mesh):
    sizes = {"row": mesh.shape["row"], "col": mesh.shape["col"]}
    return jax.shard_map(
        functools.partial(local, sizes),
        mesh=mesh,
        in_specs=(
            P("rep", "col", "row", None),
            P("rep", "col", "row", None),
            P(),
            P(),
            P(),
            P(),
            P(),
        ),
        out_specs=(P("rep", "col", "row", None), P("rep", None), P("rep", None)),
        check_vma=False,
    )
```

time: 552 us -> 309 us (0.56); the launches traced: 542 us -> 308 us
  matrix products: 191 us -> 0 us
  Pallas kernels: 0 us -> 187 us
  local copies, waits for them, and re-layouts: 120 us -> 20.8 us
  blocking collectives: 76.3 us -> 0 us
  waiting for transfers between devices: 83.2 us -> 48.6 us
  other arithmetic: 34.7 us -> 1.1 us
  starting transfers between devices: 35.2 us -> 50 us
    dot_general x22 -> x0, matrix products: 191 us -> none  [the longest x4 59.6 us: closure_backward(): lax.dot_general(features, back_pre, (((1,), (1,)), ((), ())), preferred_e...]
    pallas_call x0 -> x8, Pallas kernels: none -> 187 us  [the longest x3 87.9 us: closure_forward(): pl.pallas_call(functools.partial(forward_kernel, nat, chunked), grid=(z,)...]
    psum x1 -> x0, blocking collectives: 76.3 us -> none  [local(): grad_w_in, grad_w_out = lax.psum((totals[0], totals[1]), ('row', 'col'))]
    ppermute x6 -> x4, waiting for transfers between devices: 69.6 us -> 17.8 us  [shift(): return lax.ppermute(field, axis, pairs)]
    while x40 -> x0, local copies, waits for them, and re-layouts: 32.6 us -> none
    convert_element_type x7 -> x1, local copies, waits for them, and re-layouts: 25.3 us -> 0.08 us  [local(): eye = jnp.eye(ROWS, dtype=BF16)]
    all_to_all x6 -> x0, local copies, waits for them, and re-layouts: 22.3 us -> none  [the longest x2 7.48 us: local(): lax.all_to_all(residual, 'row', split_axis=3, concat_axis=2, tiled=True)]
    all_to_all x5, waiting for transfers between devices: 13.6 us -> 30.9 us  [swap(): lax.all_to_all(chunks, 'row', split_axis=0, concat_axis=0, tiled=True)]
  transfers between devices with their start and end apart: 11 -> 9, of which waited for: 4 -> 5; matrix products, arithmetic and copies ran while one was open for 25% -> 4% of each run, Pallas kernels for 0% -> 20%
where the time goes in v1:
time: 309 us; the launch traced here: 308 us
  Pallas kernels  187 us (61%)
  starting transfers between devices  50 us (16%)
  waiting for transfers between devices  48.6 us (16%)
  local copies, waits for them, and re-layouts  20.8 us (7%)
    pallas_call x3, Pallas kernels, closure_forward(): pl.pallas_call(functools.partial(forward_kernel, nat, chunked), grid=(z,)...  87.9 us
    pallas_call x1, Pallas kernels, local(): pl.pallas_call(functools.partial(backward_kernel, scale), grid=(y // ROWS...  57.4 us
    all_to_all x5, waiting for transfers between devices, swap(): lax.all_to_all(chunks, 'row', split_axis=0, concat_axis=0, tiled=True)  30.9 us
    ppermute x4, starting transfers between devices, shift(): return lax.ppermute(field, axis, pairs)  28.9 us
    pallas_call x1, Pallas kernels, reduce_all(): pl.pallas_call(functools.partial(reduce_kernel, sizes), out_shape=jax.Sha...  22.5 us
    all_to_all x5, starting transfers between devices, swap(): lax.all_to_all(chunks, 'row', split_axis=0, concat_axis=0, tiled=True)  21.1 us
    ppermute x4, waiting for transfers between devices, shift(): return lax.ppermute(field, axis, pairs)  17.8 us
    unnamed x28, local copies, waits for them, and re-layouts  9.99 us
  transfers between devices with their start and end apart: 9, of which 5 were waited for; matrix products, arithmetic and copies ran while one was open for 4% of the time, Pallas kernels for 20%

profile of v1, /device:TPU:0, one launch (start us, length us, event | category | flops | bytes accessed | tf_op | source)
XLA Modules:
  0.0 308.1 jit_solution(4880901696992450214)
XLA Ops:
  4.0 35.4 %closure_forward.3 = (bf16[5,4,128,512]{3,2,1,0:T(8,128)(2,1)}, bf16[4,3,4,128,128]{4,3,2,1,0:T(8,128)(2,1)}) custom-call(bf16[3,4,128,512]{3,2,1,0:T(8,128)(2,1)} %v_ref.5, bf16[1024,144]{1,0:T(8,128)(2,1)} %copy.15.win_ref, bf16[96,1024]{1,0:T(8,128)(2,1)} %mul.83.wout_ref), custom_call_target="tpu_custom_call" | custom-call | flops 5033164800 | bytes 5242880 | tf_op jit(solution)/shard_map/closure_forward/pallas_call | solution.py:73
  39.5 5.3 %all-to-all-start = ((bf16[4,3,4,128,128]{4,3,2,1,0:T(8,128)(2,1)}), bf16[4,3,4,128,128]{4,3,2,1,0:T(8,128)(2,1)}, u32[]{:S(2)}, u32[]{:S(2)}) async-start(bf16[4,3,4,128,128]{4,3,2,1,0:T(8,128)(2,1)} %get-tuple-element.9), calls=%async_computation | async-start | bytes 3145728 | tf_op jit(solution)/shard_map/all_to_all | solution.py:313
  47.3 17.5 %all-to-all-done.s_ref = bf16[4,3,4,128,128]{4,3,2,1,0:T(8,128)(2,1)} async-done(((bf16[4,3,4,128,128]{4,3,2,1,0:T(8,128)(2,1)}), bf16[4,3,4,128,128]{4,3,2,1,0:T(8,128)(2,1)}, u32[]{:S(2)}, u32[]{:S(2)}) %all-to-all-start) | async-done | bytes 1572896 | tf_op jit(solution)/shard_map/all_to_all | solution.py:313
  64.8 3.6 %all-to-all-start.1 = ((bf16[4,3,4,128,128]{4,3,2,1,0:T(8,128)(2,1)}), bf16[4,3,4,128,128]{4,3,2,1,0:T(8,128)(2,1)S(1)}, u32[]{:S(2)}, u32[]{:S(2)}) async-start(bf16[4,3,4,128,128]{4,3,2,1,0:T(8,128)(2,1)} %bitcast.2), calls=%async_computation.1 | async-start | bytes 3145728 | tf_op jit(solution)/shard_map/all_to_all | solution.py:313
  68.3 1.7 fusion.2
  70.1 1.8 collective-permute-start
  71.9 2.0 collective-permute-start.1
  73.9 13.4 %all-to-all-done.1.v_ref = bf16[4,3,4,128,128]{4,3,2,1,0:T(8,128)(2,1)S(1)} async-done(((bf16[4,3,4,128,128]{4,3,2,1,0:T(8,128)(2,1)}), bf16[4,3,4,128,128]{4,3,2,1,0:T(8,128)(2,1)S(1)}, u32[]{:S(2)}, u32[]{:S(2)}) %all-to-all-start.1) | async-done | bytes 1572896 | tf_op jit(solution)/shard_map/all_to_all | solution.py:313
  88.4 5.1 %pencil.2 = bf16[4,3,4,128,128]{4,3,2,1,0:T(8,128)(2,1)} custom-call(bf16[512,512]{1,0:T(8,128)(2,1)} %dy_ref.1, bf16[4,3,4,128,128]{4,3,2,1,0:T(8,128)(2,1)} %all-to-all-done.s_ref, bf16[4,3,4,128,128]{4,3,2,1,0:T(8,128)(2,1)} %copy-done.5), custom_call_target="tpu_custom_call" | custom-call | tf_op jit(solution)/shard_map/pencil/pallas_call | solution.py:112
  93.5 3.7 %all-to-all-start.2 = ((bf16[4,3,4,128,128]{4,3,2,1,0:T(8,128)(2,1)}), bf16[4,3,4,128,128]{4,3,2,1,0:T(8,128)(2,1)S(1)}, u32[]{:S(2)}, u32[]{:S(2)}) async-start(bf16[4,3,4,128,128]{4,3,2,1,0:T(8,128)(2,1)} %pencil.2), calls=%async_computation.2 | async-start | bytes 3145728 | tf_op jit(solution)/shard_map/all_to_all | solution.py:313
  99.4 1.7 collective-permute-done.v_ref.lo_ref
  101.1 26.2 %closure_forward.4.slo_ref = bf16[3,3,128,512]{3,2,1,0:T(8,128)(2,1)} custom-call(bf16[3,3,128,512]{3,2,1,0:T(8,128)(2,1)} %collective-permute-done.v_ref.lo_ref, bf16[1024,144]{1,0:T(8,128)(2,1)} %copy.15.win_ref, bf16[48,1024]{1,0:T(8,128)(2,1)} %copy-done.8), custom_call_target="tpu_custom_call" | custom-call | flops 3774873600 | bytes 3932160 | tf_op jit(solution)/shard_map/closure_forward/pallas_call | solution.py:73
  127.3 26.3 %closure_forward.5.shi_ref = bf16[3,3,128,512]{3,2,1,0:T(8,128)(2,1)} custom-call(bf16[3,3,128,512]{3,2,1,0:T(8,128)(2,1)} %collective-permute-done.1.v_ref.hi_ref, bf16[1024,144]{1,0:T(8,128)(2,1)} %copy.15.win_ref, bf16[48,1024]{1,0:T(8,128)(2,1)} %copy-done.8), custom_call_target="tpu_custom_call" | custom-call | flops 3774873600 | bytes 3932160 | tf_op jit(solution)/shard_map/closure_forward/pallas_call | solution.py:73
  154.7 9.3 %advance.1 = (bf16[3,4,128,512]{3,2,1,0:T(8,128)(2,1)}, bf16[3,4,128,512]{3,2,1,0:T(8,128)(2,1)}, bf16[4,3,4,128,128]{4,3,2,1,0:T(8,128)(2,1)}) custom-call(f32[10]{0:T(128)} %dynamic_slice.3.metric_ref, bf16[3,4,128,512]{3,2,1,0:T(8,128)(2,1)} %v_ref.5, bf16[3,3,128,512]{3,2,1,0:T(8,128)(2,1)} %collective-permute-done.v_ref.lo_ref, ...), custom_call_target="tpu_custom_call" | custom-call | tf_op jit(solution)/shard_map/advance/pallas_call | solution.py:355
  164.1 4.3 %all-to-all-start.3 = ((bf16[4,3,4,128,128]{4,3,2,1,0:T(8,128)(2,1)}), bf16[4,3,4,128,128]{4,3,2,1,0:T(8,128)(2,1)S(1)}, u32[]{:S(2)}, u32[]{:S(2)}) async-start(bf16[4,3,4,128,128]{4,3,2,1,0:T(8,128)(2,1)} %get-tuple-element.12), calls=%async_computation.3 | async-start | bytes 3145728 | tf_op jit(solution)/shard_map/all_to_all | solution.py:313
  168.4 2.0 copy.21
  170.4 1.8 fusion.1
  172.7 24.5 %collective-permute-start.3 = (bf16[3,3,128,512]{3,2,1,0:T(8,128)(2,1)}, bf16[3,3,128,512]{3,2,1,0:T(8,128)(2,1)}, u32[]{:S(2)}, u32[]{:S(2)}) collective-permute-start(bf16[3,3,128,512]{3,2,1,0:T(8,128)(2,1)} %get-tuple-element.13), channel_id=1, source_target_pairs={{1,0},{2,1},{3,2},{0,3},{5,4},{6,5},{7,6},{4,7},{9,8},{10,9},{11,1... | collective-permute-start | bytes 3538952 | tf_op jit(solution)/shard_map/ppermute | solution.py:302
  198.4 4.6 %pencil.3 = bf16[4,3,4,128,128]{4,3,2,1,0:T(8,128)(2,1)} custom-call(bf16[512,512]{1,0:T(8,128)(2,1)} %bitcast.27, bf16[4,3,4,128,128]{4,3,2,1,0:T(8,128)(2,1)} %copy-done.4), custom_call_target="tpu_custom_call" | custom-call | tf_op jit(solution)/shard_map/pencil/pallas_call | solution.py:112
  203.0 4.2 %all-to-all-start.4 = ((bf16[4,3,4,128,128]{4,3,2,1,0:T(8,128)(2,1)}), bf16[4,3,4,128,128]{4,3,2,1,0:T(8,128)(2,1)S(1)}, u32[]{:S(2)}, u32[]{:S(2)}) async-start(bf16[4,3,4,128,128]{4,3,2,1,0:T(8,128)(2,1)} %pencil.3), calls=%async_computation.4 | async-start | bytes 3145728 | tf_op jit(solution)/shard_map/all_to_all | solution.py:313
  208.4 4.1 %collective-permute-done.2.rlo_ref = bf16[3,3,128,512]{3,2,1,0:T(8,128)(2,1)S(1)} collective-permute-done((bf16[3,3,128,512]{3,2,1,0:T(8,128)(2,1)}, bf16[3,3,128,512]{3,2,1,0:T(8,128)(2,1)S(1)}, u32[]{:S(2)}, u32[]{:S(2)}) %collective-permute-start.2) | collective-permute-done | bytes 1179680 | tf_op jit(solution)/shard_map/ppermute | solution.py:302
  212.5 12.0 %collective-permute-done.3.rhi_ref = bf16[3,3,128,512]{3,2,1,0:T(8,128)(2,1)} collective-permute-done((bf16[3,3,128,512]{3,2,1,0:T(8,128)(2,1)}, bf16[3,3,128,512]{3,2,1,0:T(8,128)(2,1)}, u32[]{:S(2)}, u32[]{:S(2)}) %collective-permute-start.3) | collective-permute-done | bytes 1179680 | tf_op jit(solution)/shard_map/ppermute | solution.py:302
  225.7 57.4 %closure_backward.1.x_ref = f32[16,64]{1,0:T(8,128)} custom-call(f32[10]{0:T(128)} %dynamic_slice.3.metric_ref, bf16[3,4,128,512]{3,2,1,0:T(8,128)(2,1)} %v_ref.5, bf16[3,4,128,512]{3,2,1,0:T(8,128)(2,1)} %get-tuple-element.11.r_ref, bf16[3,3,128,512]{3,2,1,0:T(8,128)(2,1)} %copy-done.7, bf16[3,3,128,512]{3,2,1,0:T(8,128)(2,1)} %collective-permute-done.3.rhi_ref, ...), custom_call_target="tpu_custom_call" | custom-call | tf_op jit(solution)/shard_map/closure_backward/pallas_call | solution.py:375
  283.1 22.5 %reduce_all.1 = f32[16,64]{1,0:T(8,128)} custom-call(f32[16,64]{1,0:T(8,128)} %closure_backward.1.x_ref), custom_call_target="tpu_custom_call" | custom-call | tf_op jit(solution)/shard_map/reduce_all/pallas_call | solution.py:282
  (53 shorter events, 17.0 us)
Async XLA Ops:
  0.6 2.3 copy-start.9
  39.5 5.3 %copy-start = (bf16[3,4,128,512]{3,2,1,0:T(8,128)(2,1)S(1)}, bf16[3,4,128,512]{3,2,1,0:T(8,128)(2,1)}, u32[]{:S(2)}) copy-start(bf16[3,4,128,512]{3,2,1,0:T(8,128)(2,1)} %v_ref.5) | copy-start | bytes 4718596
  39.5 25.3 %all-to-all-start = ((bf16[4,3,4,128,128]{4,3,2,1,0:T(8,128)(2,1)}), bf16[4,3,4,128,128]{4,3,2,1,0:T(8,128)(2,1)}, u32[]{:S(2)}, u32[]{:S(2)}) async-start(bf16[4,3,4,128,128]{4,3,2,1,0:T(8,128)(2,1)} %get-tuple-element.9), calls=%async_computation | async-start | bytes 3145728 | tf_op jit(solution)/shard_map/all_to_all | solution.py:313
  64.8 22.5 %all-to-all-start.1 = ((bf16[4,3,4,128,128]{4,3,2,1,0:T(8,128)(2,1)}), bf16[4,3,4,128,128]{4,3,2,1,0:T(8,128)(2,1)S(1)}, u32[]{:S(2)}, u32[]{:S(2)}) async-start(bf16[4,3,4,128,128]{4,3,2,1,0:T(8,128)(2,1)} %bitcast.2), calls=%async_computation.1 | async-start | bytes 3145728 | tf_op jit(solution)/shard_map/all_to_all | solution.py:313
  70.1 31.0 %collective-permute-start = (bf16[3,3,128,512]{3,2,1,0:T(8,128)(2,1)}, bf16[3,3,128,512]{3,2,1,0:T(8,128)(2,1)}, u32[]{:S(2)}, u32[]{:S(2)}) collective-permute-start(bf16[3,3,128,512]{3,2,1,0:T(8,128)(2,1)} %get-tuple-element.16), channel_id=1, source_target_pairs={{0,1},{1,2},{2,3},{3,0},{4,5},{5,6},{6,7},{7,4},{8,9},{9,10},{10,1... | collective-permute-start | bytes 3538952 | tf_op jit(solution)/shard_map/ppermute | solution.py:302
  71.9 55.4 %collective-permute-start.1 = (bf16[3,3,128,512]{3,2,1,0:T(8,128)(2,1)}, bf16[3,3,128,512]{3,2,1,0:T(8,128)(2,1)}, u32[]{:S(2)}, u32[]{:S(2)}) collective-permute-start(bf16[3,3,128,512]{3,2,1,0:T(8,128)(2,1)} %get-tuple-element.15), channel_id=1, source_target_pairs={{1,0},{2,1},{3,2},{0,3},{5,4},{6,5},{7,6},{4,7},{9,8},{10,9},{11,1... | collective-permute-start | bytes 3538952 | tf_op jit(solution)/shard_map/ppermute | solution.py:302
  87.3 1.1 copy-start.5
  93.5 4.1 %copy-start.6 = (bf16[512,512]{1,0:T(8,128)(2,1)S(1)}, bf16[512,512]{1,0:T(8,128)(2,1)}, u32[]{:S(2)}) copy-start(bf16[512,512]{1,0:T(8,128)(2,1)} %dx_ref.1) | copy-start | bytes 1572868
  93.5 60.0 %all-to-all-start.2 = ((bf16[4,3,4,128,128]{4,3,2,1,0:T(8,128)(2,1)}), bf16[4,3,4,128,128]{4,3,2,1,0:T(8,128)(2,1)S(1)}, u32[]{:S(2)}, u32[]{:S(2)}) async-start(bf16[4,3,4,128,128]{4,3,2,1,0:T(8,128)(2,1)} %pencil.2), calls=%async_computation.2 | async-start | bytes 3145728 | tf_op jit(solution)/shard_map/all_to_all | solution.py:313
  97.2 1.5 copy-start.10
  99.4 1.7 copy-start.8
  153.6 1.2 copy-start.2
  164.1 6.4 %copy-start.1 = (bf16[3,4,128,512]{3,2,1,0:T(8,128)(2,1)S(1)}, bf16[3,4,128,512]{3,2,1,0:T(8,128)(2,1)}, u32[]{:S(2)}) copy-start(bf16[3,4,128,512]{3,2,1,0:T(8,128)(2,1)} %get-tuple-element.11.r_ref) | copy-start | bytes 4718596
  164.1 33.2 %all-to-all-start.3 = ((bf16[4,3,4,128,128]{4,3,2,1,0:T(8,128)(2,1)}), bf16[4,3,4,128,128]{4,3,2,1,0:T(8,128)(2,1)S(1)}, u32[]{:S(2)}, u32[]{:S(2)}) async-start(bf16[4,3,4,128,128]{4,3,2,1,0:T(8,128)(2,1)} %get-tuple-element.12), calls=%async_computation.3 | async-start | bytes 3145728 | tf_op jit(solution)/shard_map/all_to_all | solution.py:313
  172.2 40.3 %collective-permute-start.2 = (bf16[3,3,128,512]{3,2,1,0:T(8,128)(2,1)}, bf16[3,3,128,512]{3,2,1,0:T(8,128)(2,1)S(1)}, u32[]{:S(2)}, u32[]{:S(2)}) collective-permute-start(bf16[3,3,128,512]{3,2,1,0:T(8,128)(2,1)} %get-tuple-element.14), channel_id=1, source_target_pairs={{0,1},{1,2},{2,3},{3,0},{4,5},{5,6},{6,7},{7,4},{8,9},{9,10},{10,1... | collective-permute-start | bytes 3538952 | tf_op jit(solution)/shard_map/ppermute | solution.py:302
  172.7 51.8 %collective-permute-start.3 = (bf16[3,3,128,512]{3,2,1,0:T(8,128)(2,1)}, bf16[3,3,128,512]{3,2,1,0:T(8,128)(2,1)}, u32[]{:S(2)}, u32[]{:S(2)}) collective-permute-start(bf16[3,3,128,512]{3,2,1,0:T(8,128)(2,1)} %get-tuple-element.13), channel_id=1, source_target_pairs={{1,0},{2,1},{3,2},{0,3},{5,4},{6,5},{7,6},{4,7},{9,8},{10,9},{11,1... | collective-permute-start | bytes 3538952 | tf_op jit(solution)/shard_map/ppermute | solution.py:302
  197.3 1.2 copy-start.4
  203.0 21.5 %all-to-all-start.4 = ((bf16[4,3,4,128,128]{4,3,2,1,0:T(8,128)(2,1)}), bf16[4,3,4,128,128]{4,3,2,1,0:T(8,128)(2,1)S(1)}, u32[]{:S(2)}, u32[]{:S(2)}) async-start(bf16[4,3,4,128,128]{4,3,2,1,0:T(8,128)(2,1)} %pencil.3), calls=%async_computation.4 | async-start | bytes 3145728 | tf_op jit(solution)/shard_map/all_to_all | solution.py:313
  212.5 12.0 %copy-start.7 = (bf16[3,3,128,512]{3,2,1,0:T(8,128)(2,1)}, bf16[3,3,128,512]{3,2,1,0:T(8,128)(2,1)S(1)}, u32[]{:S(2)}) copy-start(bf16[3,3,128,512]{3,2,1,0:T(8,128)(2,1)S(1)} %collective-permute-done.2.rlo_ref) | copy-start | bytes 3538948
  224.5 1.2 copy-start.3

commit v2 on v1

--- a/solution.py
+++ b/solution.py
@@ -8,6 +8,7 @@
 from jax.experimental.pallas import tpu as pltpu
 from jax.sharding import PartitionSpec as P
 
+
 COEFS = (0.75, -0.15, 1.0 / 60.0)
 STEP_SIZE = 0.3
 ROWS = 16
@@ -34,7 +35,7 @@
 
 def forward_kernel(nat, chunked, v_ref, win_ref, wout_ref, *outs):
     y_cells = v_ref.shape[2]
-    total_rows, quarter = win_ref.shape[0], win_ref.shape[0] // 4
+    quarter = win_ref.shape[0] // 4
 
     def body(g, carry):
         rows = pl.ds(pl.multiple_of(g * ROWS, ROWS), ROWS)
@@ -43,7 +44,8 @@
         for q in range(4):
             part = slice(q * quarter, (q + 1) * quarter)
             half = dot(win_ref[part, :], feats)
-            hidden = (half + half * jnp.tanh(half)).astype(BF16)
+            t = jnp.tanh(half.astype(BF16)).astype(F32)
+            hidden = (half + half * t).astype(BF16)
             term = dot(wout_ref[:, part], hidden)
             stress = term if stress is None else stress + term
         stress = stress.astype(BF16)
@@ -196,12 +198,11 @@
         up = up_ref[k]
         for q in range(4):
             part = slice(q * quarter, (q + 1) * quarter)
-            half = dot(win_ref[part, :], feats)
+            half = dot(win_ref[part, :], feats).astype(BF16)
             t = jnp.tanh(half)
-            one = 1.0 + t
-            hidden = (half * one).astype(BF16)
-            back_hidden = dot(wot_ref[part, :], up)
-            back = (back_hidden * (one * (1.0 + half * (1.0 - t)))).astype(BF16)
+            hidden = half + half * t
+            back_hidden = dot(wot_ref[part, :], up).astype(BF16)
+            back = back_hidden * (1 + t + half * (1 - t * t))
             gout_ref[:, part] += dot_nt(up, hidden)
             gin_ref[:, part] += dot_nt(feats, back)
         return carry
@@ -313,15 +314,19 @@
     return lax.all_to_all(chunks, "row", split_axis=0, concat_axis=0, tiled=True)
 
 
-def local(sizes, velocity, target, w_in, w_out, diff_x, diff_y, metric_z):
+def local(sizes, *args):
+    return step(sizes, *args)
+
+
+def step(sizes, velocity, target, w_in, w_out, diff_x, diff_y, metric_z):
     n_row, n_col = sizes["row"], sizes["col"]
     _, z, y, x = velocity.shape
     y_total, z_total = diff_y.shape[0], metric_z.shape[0]
     ch = w_in.shape[1]
     w = x // n_row
     v_chunks = velocity.reshape(3, z, y, n_row, w).transpose(3, 0, 1, 2, 4)
+    v_low, v_high = halo(velocity, n_col)
     v_pencil = swap(v_chunks)
-    v_low, v_high = halo(velocity, n_col)
 
     eye = jnp.eye(ROWS, dtype=BF16)
     half_in = w_in.T * jnp.asarray(0.5, BF16)
@@ -334,7 +339,9 @@
     stress, sy_chunks = closure_forward(
         velocity, win, wout, (XX, XY, XZ, YZ, ZZ), (XY, YY, YZ), n_row
     )
-    part_y = swap(pencil_call(pencil_kernel, diff_y, swap(sy_chunks), v_pencil))
+    s_pencil = swap(sy_chunks)
+    part_y = pencil_call(pencil_kernel, diff_y, s_pencil, v_pencil)
+    part_y = swap(part_y)
     s_low = closure_forward(v_low, win, wout_z, (0, 1, 2), (), 1)[0]
     s_high = closure_forward(v_high, win, wout_z, (0, 1, 2), (), 1)[0]
 

time: 309 us -> 312 us (level)
    pallas_call x3, Pallas kernels: 87.9 us -> 91.7 us  [closure_forward(): pl.pallas_call(functools.partial(forward_kernel, nat, chunked), grid=(z,)...]
  transfers between devices with their start and end apart: 9 -> 9, of which waited for: 5 -> 5; matrix products, arithmetic and copies ran while one was open for 4% -> 4% of each run, Pallas kernels for 20% -> 21%
where the time goes in v2:
time: 312 us; the launch traced here: 311 us
  Pallas kernels  190 us (61%)
  starting transfers between devices  50 us (16%)
  waiting for transfers between devices  48.6 us (16%)
  local copies, waits for them, and re-layouts  20.8 us (7%)
    pallas_call x3, Pallas kernels, closure_forward(): pl.pallas_call(functools.partial(forward_kernel, nat, chunked), grid=(z,)...  91.7 us
    pallas_call x1, Pallas kernels, step(): pl.pallas_call(functools.partial(backward_kernel, scale), grid=(y // ROWS...  56.4 us
    all_to_all x5, waiting for transfers between devices, swap(): lax.all_to_all(chunks, 'row', split_axis=0, concat_axis=0, tiled=True)  30.8 us
    ppermute x4, starting transfers between devices, shift(): return lax.ppermute(field, axis, pairs)  28.9 us
    pallas_call x1, Pallas kernels, reduce_all(): pl.pallas_call(functools.partial(reduce_kernel, sizes), out_shape=jax.Sha...  22.5 us
    all_to_all x5, starting transfers between devices, swap(): lax.all_to_all(chunks, 'row', split_axis=0, concat_axis=0, tiled=True)  21.1 us
    ppermute x4, waiting for transfers between devices, shift(): return lax.ppermute(field, axis, pairs)  17.8 us
    unnamed x28, local copies, waits for them, and re-layouts  9.99 us
  transfers between devices with their start and end apart: 9, of which 5 were waited for; matrix products, arithmetic and copies ran while one was open for 4% of the time, Pallas kernels for 21%

profile of v2, /device:TPU:0, one launch (start us, length us, event | category | flops | bytes accessed | tf_op | source)
XLA Modules:
  0.0 310.9 jit_solution(12932785805120234257)
XLA Ops:
  4.0 36.8 %closure_forward.3 = (bf16[5,4,128,512]{3,2,1,0:T(8,128)(2,1)}, bf16[4,3,4,128,128]{4,3,2,1,0:T(8,128)(2,1)}) custom-call(bf16[3,4,128,512]{3,2,1,0:T(8,128)(2,1)} %v_ref.5, bf16[1024,144]{1,0:T(8,128)(2,1)} %copy.15.win_ref, bf16[96,1024]{1,0:T(8,128)(2,1)} %mul.83.wout_ref), custom_call_target="tpu_custom_call" | custom-call | flops 5033164800 | bytes 5242880 | tf_op jit(solution)/shard_map/closure_forward/pallas_call | solution.py:75
  40.8 5.3 %all-to-all-start = ((bf16[4,3,4,128,128]{4,3,2,1,0:T(8,128)(2,1)}), bf16[4,3,4,128,128]{4,3,2,1,0:T(8,128)(2,1)}, u32[]{:S(2)}, u32[]{:S(2)}) async-start(bf16[4,3,4,128,128]{4,3,2,1,0:T(8,128)(2,1)} %get-tuple-element.9), calls=%async_computation | async-start | bytes 3145728 | tf_op jit(solution)/shard_map/all_to_all | solution.py:314
  48.7 17.5 %all-to-all-done.s_ref = bf16[4,3,4,128,128]{4,3,2,1,0:T(8,128)(2,1)} async-done(((bf16[4,3,4,128,128]{4,3,2,1,0:T(8,128)(2,1)}), bf16[4,3,4,128,128]{4,3,2,1,0:T(8,128)(2,1)}, u32[]{:S(2)}, u32[]{:S(2)}) %all-to-all-start) | async-done | bytes 1572896 | tf_op jit(solution)/shard_map/all_to_all | solution.py:314
  66.1 3.6 %all-to-all-start.1 = ((bf16[4,3,4,128,128]{4,3,2,1,0:T(8,128)(2,1)}), bf16[4,3,4,128,128]{4,3,2,1,0:T(8,128)(2,1)S(1)}, u32[]{:S(2)}, u32[]{:S(2)}) async-start(bf16[4,3,4,128,128]{4,3,2,1,0:T(8,128)(2,1)} %bitcast.2), calls=%async_computation.1 | async-start | bytes 3145728 | tf_op jit(solution)/shard_map/all_to_all | solution.py:314
  69.7 1.7 fusion.2
  71.4 1.8 collective-permute-start
  73.2 2.0 collective-permute-start.1
  75.2 13.4 %all-to-all-done.1.v_ref = bf16[4,3,4,128,128]{4,3,2,1,0:T(8,128)(2,1)S(1)} async-done(((bf16[4,3,4,128,128]{4,3,2,1,0:T(8,128)(2,1)}), bf16[4,3,4,128,128]{4,3,2,1,0:T(8,128)(2,1)S(1)}, u32[]{:S(2)}, u32[]{:S(2)}) %all-to-all-start.1) | async-done | bytes 1572896 | tf_op jit(solution)/shard_map/all_to_all | solution.py:314
  89.8 5.1 %pencil.2 = bf16[4,3,4,128,128]{4,3,2,1,0:T(8,128)(2,1)} custom-call(bf16[512,512]{1,0:T(8,128)(2,1)} %dy_ref.1, bf16[4,3,4,128,128]{4,3,2,1,0:T(8,128)(2,1)} %all-to-all-done.s_ref, bf16[4,3,4,128,128]{4,3,2,1,0:T(8,128)(2,1)} %copy-done.5), custom_call_target="tpu_custom_call" | custom-call | tf_op jit(solution)/shard_map/pencil/pallas_call | solution.py:114
  94.9 3.7 %all-to-all-start.2 = ((bf16[4,3,4,128,128]{4,3,2,1,0:T(8,128)(2,1)}), bf16[4,3,4,128,128]{4,3,2,1,0:T(8,128)(2,1)S(1)}, u32[]{:S(2)}, u32[]{:S(2)}) async-start(bf16[4,3,4,128,128]{4,3,2,1,0:T(8,128)(2,1)} %pencil.2), calls=%async_computation.2 | async-start | bytes 3145728 | tf_op jit(solution)/shard_map/all_to_all | solution.py:314
  100.7 1.7 collective-permute-done.v_ref.lo_ref
  102.4 27.4 %closure_forward.4.slo_ref = bf16[3,3,128,512]{3,2,1,0:T(8,128)(2,1)} custom-call(bf16[3,3,128,512]{3,2,1,0:T(8,128)(2,1)} %collective-permute-done.v_ref.lo_ref, bf16[1024,144]{1,0:T(8,128)(2,1)} %copy.15.win_ref, bf16[48,1024]{1,0:T(8,128)(2,1)} %copy-done.8), custom_call_target="tpu_custom_call" | custom-call | flops 3774873600 | bytes 3932160 | tf_op jit(solution)/shard_map/closure_forward/pallas_call | solution.py:75
  129.9 27.5 %closure_forward.5.shi_ref = bf16[3,3,128,512]{3,2,1,0:T(8,128)(2,1)} custom-call(bf16[3,3,128,512]{3,2,1,0:T(8,128)(2,1)} %collective-permute-done.1.v_ref.hi_ref, bf16[1024,144]{1,0:T(8,128)(2,1)} %copy.15.win_ref, bf16[48,1024]{1,0:T(8,128)(2,1)} %copy-done.8), custom_call_target="tpu_custom_call" | custom-call | flops 3774873600 | bytes 3932160 | tf_op jit(solution)/shard_map/closure_forward/pallas_call | solution.py:75
  158.5 9.3 %advance.1 = (bf16[3,4,128,512]{3,2,1,0:T(8,128)(2,1)}, bf16[3,4,128,512]{3,2,1,0:T(8,128)(2,1)}, bf16[4,3,4,128,128]{4,3,2,1,0:T(8,128)(2,1)}) custom-call(f32[10]{0:T(128)} %dynamic_slice.3.metric_ref, bf16[3,4,128,512]{3,2,1,0:T(8,128)(2,1)} %v_ref.5, bf16[3,3,128,512]{3,2,1,0:T(8,128)(2,1)} %collective-permute-done.v_ref.lo_ref, ...), custom_call_target="tpu_custom_call" | custom-call | tf_op jit(solution)/shard_map/advance/pallas_call | solution.py:362
  167.8 4.3 %all-to-all-start.3 = ((bf16[4,3,4,128,128]{4,3,2,1,0:T(8,128)(2,1)}), bf16[4,3,4,128,128]{4,3,2,1,0:T(8,128)(2,1)S(1)}, u32[]{:S(2)}, u32[]{:S(2)}) async-start(bf16[4,3,4,128,128]{4,3,2,1,0:T(8,128)(2,1)} %get-tuple-element.12), calls=%async_computation.3 | async-start | bytes 3145728 | tf_op jit(solution)/shard_map/all_to_all | solution.py:314
  172.1 2.0 copy.21
  174.2 1.8 fusion.1
  176.5 24.5 %collective-permute-start.3 = (bf16[3,3,128,512]{3,2,1,0:T(8,128)(2,1)}, bf16[3,3,128,512]{3,2,1,0:T(8,128)(2,1)}, u32[]{:S(2)}, u32[]{:S(2)}) collective-permute-start(bf16[3,3,128,512]{3,2,1,0:T(8,128)(2,1)} %get-tuple-element.13), channel_id=1, source_target_pairs={{1,0},{2,1},{3,2},{0,3},{5,4},{6,5},{7,6},{4,7},{9,8},{10,9},{11,1... | collective-permute-start | bytes 3538952 | tf_op jit(solution)/shard_map/ppermute | solution.py:303
  202.2 4.6 %pencil.3 = bf16[4,3,4,128,128]{4,3,2,1,0:T(8,128)(2,1)} custom-call(bf16[512,512]{1,0:T(8,128)(2,1)} %bitcast.27, bf16[4,3,4,128,128]{4,3,2,1,0:T(8,128)(2,1)} %copy-done.4), custom_call_target="tpu_custom_call" | custom-call | tf_op jit(solution)/shard_map/pencil/pallas_call | solution.py:114
  206.8 4.2 %all-to-all-start.4 = ((bf16[4,3,4,128,128]{4,3,2,1,0:T(8,128)(2,1)}), bf16[4,3,4,128,128]{4,3,2,1,0:T(8,128)(2,1)S(1)}, u32[]{:S(2)}, u32[]{:S(2)}) async-start(bf16[4,3,4,128,128]{4,3,2,1,0:T(8,128)(2,1)} %pencil.3), calls=%async_computation.4 | async-start | bytes 3145728 | tf_op jit(solution)/shard_map/all_to_all | solution.py:314
  212.2 4.0 %collective-permute-done.2.rlo_ref = bf16[3,3,128,512]{3,2,1,0:T(8,128)(2,1)S(1)} collective-permute-done((bf16[3,3,128,512]{3,2,1,0:T(8,128)(2,1)}, bf16[3,3,128,512]{3,2,1,0:T(8,128)(2,1)S(1)}, u32[]{:S(2)}, u32[]{:S(2)}) %collective-permute-start.2) | collective-permute-done | bytes 1179680 | tf_op jit(solution)/shard_map/ppermute | solution.py:303
  216.3 12.0 %collective-permute-done.3.rhi_ref = bf16[3,3,128,512]{3,2,1,0:T(8,128)(2,1)} collective-permute-done((bf16[3,3,128,512]{3,2,1,0:T(8,128)(2,1)}, bf16[3,3,128,512]{3,2,1,0:T(8,128)(2,1)}, u32[]{:S(2)}, u32[]{:S(2)}) %collective-permute-start.3) | collective-permute-done | bytes 1179680 | tf_op jit(solution)/shard_map/ppermute | solution.py:303
  229.5 56.4 %closure_backward.1.x_ref = f32[16,64]{1,0:T(8,128)} custom-call(f32[10]{0:T(128)} %dynamic_slice.3.metric_ref, bf16[3,4,128,512]{3,2,1,0:T(8,128)(2,1)} %v_ref.5, bf16[3,4,128,512]{3,2,1,0:T(8,128)(2,1)} %get-tuple-element.11.r_ref, bf16[3,3,128,512]{3,2,1,0:T(8,128)(2,1)} %copy-done.7, bf16[3,3,128,512]{3,2,1,0:T(8,128)(2,1)} %collective-permute-done.3.rhi_ref, ...), custom_call_target="tpu_custom_call" | custom-call | tf_op jit(solution)/shard_map/closure_backward/pallas_call | solution.py:382
  285.9 22.5 %reduce_all.1 = f32[16,64]{1,0:T(8,128)} custom-call(f32[16,64]{1,0:T(8,128)} %closure_backward.1.x_ref), custom_call_target="tpu_custom_call" | custom-call | tf_op jit(solution)/shard_map/reduce_all/pallas_call | solution.py:283
  (53 shorter events, 17.0 us)
Async XLA Ops:
  0.6 2.3 copy-start.9
  40.8 5.3 %copy-start = (bf16[3,4,128,512]{3,2,1,0:T(8,128)(2,1)S(1)}, bf16[3,4,128,512]{3,2,1,0:T(8,128)(2,1)}, u32[]{:S(2)}) copy-start(bf16[3,4,128,512]{3,2,1,0:T(8,128)(2,1)} %v_ref.5) | copy-start | bytes 4718596
  40.8 25.3 %all-to-all-start = ((bf16[4,3,4,128,128]{4,3,2,1,0:T(8,128)(2,1)}), bf16[4,3,4,128,128]{4,3,2,1,0:T(8,128)(2,1)}, u32[]{:S(2)}, u32[]{:S(2)}) async-start(bf16[4,3,4,128,128]{4,3,2,1,0:T(8,128)(2,1)} %get-tuple-element.9), calls=%async_computation | async-start | bytes 3145728 | tf_op jit(solution)/shard_map/all_to_all | solution.py:314
  66.1 22.5 %all-to-all-start.1 = ((bf16[4,3,4,128,128]{4,3,2,1,0:T(8,128)(2,1)}), bf16[4,3,4,128,128]{4,3,2,1,0:T(8,128)(2,1)S(1)}, u32[]{:S(2)}, u32[]{:S(2)}) async-start(bf16[4,3,4,128,128]{4,3,2,1,0:T(8,128)(2,1)} %bitcast.2), calls=%async_computation.1 | async-start | bytes 3145728 | tf_op jit(solution)/shard_map/all_to_all | solution.py:314
  71.4 31.0 %collective-permute-start = (bf16[3,3,128,512]{3,2,1,0:T(8,128)(2,1)}, bf16[3,3,128,512]{3,2,1,0:T(8,128)(2,1)}, u32[]{:S(2)}, u32[]{:S(2)}) collective-permute-start(bf16[3,3,128,512]{3,2,1,0:T(8,128)(2,1)} %get-tuple-element.16), channel_id=1, source_target_pairs={{0,1},{1,2},{2,3},{3,0},{4,5},{5,6},{6,7},{7,4},{8,9},{9,10},{10,1... | collective-permute-start | bytes 3538952 | tf_op jit(solution)/shard_map/ppermute | solution.py:303
  73.2 56.6 %collective-permute-start.1 = (bf16[3,3,128,512]{3,2,1,0:T(8,128)(2,1)}, bf16[3,3,128,512]{3,2,1,0:T(8,128)(2,1)}, u32[]{:S(2)}, u32[]{:S(2)}) collective-permute-start(bf16[3,3,128,512]{3,2,1,0:T(8,128)(2,1)} %get-tuple-element.15), channel_id=1, source_target_pairs={{1,0},{2,1},{3,2},{0,3},{5,4},{6,5},{7,6},{4,7},{9,8},{10,9},{11,1... | collective-permute-start | bytes 3538952 | tf_op jit(solution)/shard_map/ppermute | solution.py:303
  88.6 1.1 copy-start.5
  94.9 4.1 %copy-start.6 = (bf16[512,512]{1,0:T(8,128)(2,1)S(1)}, bf16[512,512]{1,0:T(8,128)(2,1)}, u32[]{:S(2)}) copy-start(bf16[512,512]{1,0:T(8,128)(2,1)} %dx_ref.1) | copy-start | bytes 1572868
  94.9 62.4 %all-to-all-start.2 = ((bf16[4,3,4,128,128]{4,3,2,1,0:T(8,128)(2,1)}), bf16[4,3,4,128,128]{4,3,2,1,0:T(8,128)(2,1)S(1)}, u32[]{:S(2)}, u32[]{:S(2)}) async-start(bf16[4,3,4,128,128]{4,3,2,1,0:T(8,128)(2,1)} %pencil.2), calls=%async_computation.2 | async-start | bytes 3145728 | tf_op jit(solution)/shard_map/all_to_all | solution.py:314
  98.6 1.5 copy-start.10
  100.7 1.7 copy-start.8
  157.3 1.2 copy-start.2
  167.8 6.4 %copy-start.1 = (bf16[3,4,128,512]{3,2,1,0:T(8,128)(2,1)S(1)}, bf16[3,4,128,512]{3,2,1,0:T(8,128)(2,1)}, u32[]{:S(2)}) copy-start(bf16[3,4,128,512]{3,2,1,0:T(8,128)(2,1)} %get-tuple-element.11.r_ref) | copy-start | bytes 4718596
  167.8 33.2 %all-to-all-start.3 = ((bf16[4,3,4,128,128]{4,3,2,1,0:T(8,128)(2,1)}), bf16[4,3,4,128,128]{4,3,2,1,0:T(8,128)(2,1)S(1)}, u32[]{:S(2)}, u32[]{:S(2)}) async-start(bf16[4,3,4,128,128]{4,3,2,1,0:T(8,128)(2,1)} %get-tuple-element.12), calls=%async_computation.3 | async-start | bytes 3145728 | tf_op jit(solution)/shard_map/all_to_all | solution.py:314
  175.9 40.3 %collective-permute-start.2 = (bf16[3,3,128,512]{3,2,1,0:T(8,128)(2,1)}, bf16[3,3,128,512]{3,2,1,0:T(8,128)(2,1)S(1)}, u32[]{:S(2)}, u32[]{:S(2)}) collective-permute-start(bf16[3,3,128,512]{3,2,1,0:T(8,128)(2,1)} %get-tuple-element.14), channel_id=1, source_target_pairs={{0,1},{1,2},{2,3},{3,0},{4,5},{5,6},{6,7},{7,4},{8,9},{9,10},{10,1... | collective-permute-start | bytes 3538952 | tf_op jit(solution)/shard_map/ppermute | solution.py:303
  176.5 51.8 %collective-permute-start.3 = (bf16[3,3,128,512]{3,2,1,0:T(8,128)(2,1)}, bf16[3,3,128,512]{3,2,1,0:T(8,128)(2,1)}, u32[]{:S(2)}, u32[]{:S(2)}) collective-permute-start(bf16[3,3,128,512]{3,2,1,0:T(8,128)(2,1)} %get-tuple-element.13), channel_id=1, source_target_pairs={{1,0},{2,1},{3,2},{0,3},{5,4},{6,5},{7,6},{4,7},{9,8},{10,9},{11,1... | collective-permute-start | bytes 3538952 | tf_op jit(solution)/shard_map/ppermute | solution.py:303
  201.0 1.2 copy-start.4
  206.8 21.5 %all-to-all-start.4 = ((bf16[4,3,4,128,128]{4,3,2,1,0:T(8,128)(2,1)}), bf16[4,3,4,128,128]{4,3,2,1,0:T(8,128)(2,1)S(1)}, u32[]{:S(2)}, u32[]{:S(2)}) async-start(bf16[4,3,4,128,128]{4,3,2,1,0:T(8,128)(2,1)} %pencil.3), calls=%async_computation.4 | async-start | bytes 3145728 | tf_op jit(solution)/shard_map/all_to_all | solution.py:314
  216.3 12.0 %copy-start.7 = (bf16[3,3,128,512]{3,2,1,0:T(8,128)(2,1)}, bf16[3,3,128,512]{3,2,1,0:T(8,128)(2,1)S(1)}, u32[]{:S(2)}) copy-start(bf16[3,3,128,512]{3,2,1,0:T(8,128)(2,1)S(1)} %collective-permute-done.2.rlo_ref) | copy-start | bytes 3538948
  228.3 1.2 copy-start.3
